TPU v7x, 128 devices: a whole 4x4x4 slice. The times are simulated.
128 devices in a mesh: corpus: 16 (over y, z), blk: 8 (over x, core).
Axes of the slice: x: 4, y: 4, z: 4, core: 2. Of those that a mesh axis runs over, the one named last changes fastest.
Arguments:
- queries: bfloat16 [2048, 32, 128], P(('corpus', 'blk')), may hold values from -0.0625 to 0.0625
- index: bfloat16 [8192, 128, 128], P('corpus'), may hold values from -6 to 6
- cand_owner: int32 [2048, 64, 1], P(('corpus', 'blk')), may hold values from 0 to 15; in each aligned block of 1024 rows (0 to 1023, 1024 to 2047, ..., all dimensions but the last counted through in order) at most 128 rows name the same one
- cand_row: int32 [2048, 64], P(('corpus', 'blk')), may hold values from 0 to 511
- neg_row: int32 [128, 24], P(('corpus', 'blk')), may hold values from 0 to 511
- teacher: float32 [2048, 64], P(('corpus', 'blk')), may hold values from -16 to 16
Outputs:
- losses: float32 [2048], P(('corpus', 'blk'))
- query_grads: float32 [2048, 32, 128], P(('corpus', 'blk'))
Inputs may be any that keep to these rules, and one draw needn't show every extreme that they name: `cand_owner`: among the 1024 candidates of one device, no owner shard is named more than 128 times, and some owner shard is named exactly 128 times.
All inputs are finite; a program needn't handle non-finite values.
Results may differ from a plain program's by a relative error of at most 0.007.
Values may be sent and summed in bfloat16 or wider, within the bound.
A program may use at most 256 MiB of HBM per device.

v0:
```python
import jax
import jax.numpy as jnp
from jax import lax
from jax.sharding import PartitionSpec as P

inner_temp = 0.1
epsilon = 1e-06


def soft_terms(raw, inverse):
    scaled = raw * inverse
    expo = jnp.exp(scaled / inner_temp)
    totals = jnp.sum(expo, axis=-1, keepdims=True)
    score = inner_temp * jnp.sum(jnp.log(totals[..., 0]), axis=-1)
    weights = (expo / totals * inverse).astype(jnp.bfloat16)
    return (score, weights)


def tile_inverse(tiles):
    squares = jnp.einsum("pjd,pjd->pj", tiles, tiles, preferred_element_type=jnp.float32)
    return lax.rsqrt(squares + epsilon)


def pair_forward(query_tiles, passage_tiles):
    raw = jnp.einsum("pid,pjd->pij", query_tiles, passage_tiles, preferred_element_type=jnp.float32)
    return soft_terms(raw, tile_inverse(passage_tiles)[:, None, :])


def cross_forward(query_tiles, passage_tiles, inverse):
    raw = jnp.einsum(
        "qid,njd->qnij", query_tiles, passage_tiles, preferred_element_type=jnp.float32
    )
    return soft_terms(raw, inverse[None, :, None, :])


def on_device(queries, index, cand_owner, cand_row, neg_row, teacher):
    query_count = queries.shape[0]
    token_shape = queries.shape[1:]
    token_size = token_shape[0] * token_shape[1]
    cand_count = cand_row.shape[1]
    owner_count = lax.axis_size("corpus")
    cycle_count = lax.axis_size("blk")
    slot_room = (2 * query_count * cand_count + owner_count - 1) // owner_count
    highest = lax.Precision.HIGHEST
    widened = queries.astype(jnp.float32)
    radius = jnp.sqrt(jnp.sum(widened * widened, axis=-1, keepdims=True) + epsilon)
    unit_queries = widened / radius
    rounded = unit_queries.astype(jnp.bfloat16)
    owners = cand_owner.reshape(-1)
    hits = (owners[:, None] == jnp.arange(owner_count, dtype=jnp.int32)[None, :]).astype(jnp.int32)
    slots = jnp.sum((jnp.cumsum(hits, axis=0) - hits) * hits, axis=1)
    places = owners * slot_room + slots
    placer = (
        places[:, None] == jnp.arange(owner_count * slot_room, dtype=jnp.int32)[None, :]
    ).astype(jnp.float32)
    pair_query = (jnp.arange(query_count * cand_count, dtype=jnp.int32) // cand_count).astype(
        jnp.float32
    )
    pair_values = jnp.stack([pair_query, cand_row.reshape(-1).astype(jnp.float32)], axis=0)
    placed = jnp.dot(pair_values, placer, precision=highest, preferred_element_type=jnp.float32)
    send_query = placed[0].astype(jnp.int32).reshape(owner_count, slot_room)
    send_row = placed[1].astype(jnp.int32).reshape(owner_count, slot_room)
    got_query, got_row = (
        lax.all_to_all(send_query, "corpus", split_axis=0, concat_axis=0, tiled=True),
        lax.all_to_all(send_row, "corpus", split_axis=0, concat_axis=0, tiled=True),
    )
    copies = lax.all_gather(rounded, "corpus", axis=0, tiled=True)
    copy_groups = copies.reshape(owner_count, query_count, token_size)
    query_iota = jnp.arange(query_count, dtype=jnp.int32)

    def owner_weights(item):
        block, wanted, passages = item
        select = (wanted[:, None] == query_iota[None, :]).astype(jnp.bfloat16)
        picked = jnp.dot(select, block, preferred_element_type=jnp.float32).astype(jnp.bfloat16)
        tiles = index[passages]
        score, weights = pair_forward(picked.reshape((slot_room,) + token_shape), tiles)
        return (score, weights, tiles)

    def owner_full(item):
        score, weights, tiles = owner_weights(item)
        back = jnp.einsum("pij,pjd->pid", weights, tiles, preferred_element_type=jnp.float32)
        return (score, back)

    owner_score, owner_back = lax.map(owner_full, (copy_groups, got_query, got_row))
    back_scores = lax.all_to_all(owner_score, "corpus", split_axis=0, concat_axis=0, tiled=True)
    cand_scores = jnp.dot(
        placer, back_scores.reshape(-1), precision=highest, preferred_element_type=jnp.float32
    ).reshape(query_count, cand_count)
    neg_tiles = index[neg_row[0]]
    touring = lax.all_gather(rounded, "blk", axis=0, tiled=True)
    neg_inverse = tile_inverse(neg_tiles)
    grouped = touring.reshape((cycle_count, query_count) + token_shape)

    def neg_group(group):
        return cross_forward(group, neg_tiles, neg_inverse)

    tour_score, tour_weights = lax.map(neg_group, grouped)
    arrived = lax.all_to_all(tour_score, "blk", split_axis=0, concat_axis=0, tiled=True)
    neg_scores = arrived.transpose(1, 0, 2).reshape(query_count, -1)
    total = jnp.sum(jnp.exp(cand_scores), axis=1) + jnp.sum(jnp.exp(neg_scores), axis=1)
    spread = jnp.log(total)[:, None]
    log_target = teacher - jnp.log(jnp.sum(jnp.exp(teacher), axis=1, keepdims=True))
    target = jnp.exp(log_target)
    losses = jnp.sum(target * (log_target - cand_scores + spread), axis=1)
    cand_grad = jnp.exp(cand_scores - spread) - target
    neg_grad = jnp.exp(neg_scores - spread)
    send_grad = jnp.dot(
        cand_grad.reshape(-1), placer, precision=highest, preferred_element_type=jnp.float32
    )
    got_grad = lax.all_to_all(
        send_grad.reshape(owner_count, slot_room), "corpus", split_axis=0, concat_axis=0, tiled=True
    )
    grad_part = got_grad

    def add_source(item):
        back_one, grads_one, wanted_one = item
        select = (query_iota[:, None] == wanted_one[None, :]).astype(jnp.float32)
        terms = grads_one[:, None] * back_one.reshape(slot_room, token_size)
        return jnp.dot(select, terms, precision=highest, preferred_element_type=jnp.float32)

    pieces = lax.map(add_source, (owner_back, grad_part, got_query))
    cand_pull = lax.psum_scatter(
        pieces.reshape((query_count * lax.axis_size("corpus"),) + token_shape),
        "corpus",
        scatter_dimension=0,
        tiled=True,
    )
    grad_out = neg_grad.reshape(query_count, cycle_count, -1).transpose(1, 0, 2)
    grads_back = lax.all_to_all(grad_out, "blk", split_axis=0, concat_axis=0, tiled=True)
    grad_part = grads_back

    def one_group(item):
        weights_one, grads_one = item
        back = jnp.einsum(
            "qnij,njd->qnid", weights_one, neg_tiles, preferred_element_type=jnp.float32
        )
        return jnp.sum(grads_one[:, :, None, None] * back, axis=1)

    pieces = lax.map(one_group, (tour_weights, grad_part))
    neg_pull = lax.psum_scatter(
        pieces.reshape((query_count * lax.axis_size("blk"),) + token_shape),
        "blk",
        scatter_dimension=0,
        tiled=True,
    )
    pulled = cand_pull + neg_pull
    query_grads = (
        pulled - unit_queries * jnp.sum(unit_queries * pulled, axis=-1, keepdims=True)
    ) / radius
    return (losses, query_grads)


def solution(mesh):
    placed = (
        P(("corpus", "blk"), None, None),
        P("corpus", None, None),
        P(("corpus", "blk"), None, None),
        P(("corpus", "blk"), None),
        P(("corpus", "blk"), None),
        P(("corpus", "blk"), None),
    )
    return jax.shard_map(
        on_device,
        mesh=mesh,
        in_specs=placed,
        out_specs=(P(("corpus", "blk")), P(("corpus", "blk"), None, None)),
        check_vma=False,
    )
```

profile of v0, /device:TPU:0, one launch (start us, length us, event | category | flops | bytes accessed | tf_op | source)
XLA Modules:
  0.0 693.5 jit_solution(31858430924653053)
XLA Ops:
  10.8 4.5 reduce-window.6
  21.9 8.1 %all-to-all-start = ((s32[16,1,128]{2,1,0:T(1,128)}), s32[16,1,128]{2,1,0:T(1,128)S(1)}, u32[]{:S(2)}, u32[]{:S(2)}) async-start(s32[16,1,128]{2,1,0:T(1,128)} %get-tuple-element.239), calls=%async_computation | async-start | bytes 16384 | tf_op jit(solution)/shard_map/all_to_all | solution.py:64
  31.5 6.5 gather_fusion.1
  38.5 50.6 %while.46 = (s32[]{:T(128)}, f32[8,16,24]{2,1,0:T(8,128)S(1)}, bf16[8,16,24,32,128]{4,3,2,1,0:T(8,128)(2,1)}, bf16[8,16,32,128]{3,2,1,0:T(8,128)(2,1)}, bf16[24,...) while((s32[]{:T(128)}, f32[8,16,24]{2,1,0:T(8,128)S(1)}, ...), condition=%wide.region_13.14_spmd, body=%wide.region_10.13_spmd.sunk | while | flops 415236096 | bytes 16996944 | solution.py:97
  89.8 4.3 all-to-all-start.3
  94.2 5.2 all-to-all-done.3
  99.5 7.2 %all-to-all-start.1 = ((s32[16,1,128]{2,1,0:T(1,128)}), s32[16,1,128]{2,1,0:T(1,128)S(1)}, u32[]{:S(2)}, u32[]{:S(2)}) async-start(s32[16,1,128]{2,1,0:T(1,128)} %get-tuple-element.238), calls=%async_computation.1 | async-start | bytes 16384 | tf_op jit(solution)/shard_map/all_to_all | solution.py:65
  114.3 351.5 %while.48 = (s32[]{:T(128)}, f32[16,128]{1,0:T(8,128)}, f32[16,128,32,128]{3,2,1,0:T(8,128)}, s32[16,128]{1,0:T(8,128)S(1)}, bf16[16,16,4096]{2,1,0:T(8,128)(2,1...) while((s32[]{:T(128)}, f32[16,128]{1,0:T(8,128)}, ...), condition=%wide.region_8.9_spmd.clone, body=%wide.region_5.8_spmd.clone.sunk | while | flops 296226176 | bytes 65530560 | solution.py:84
  116.4 8.8 %gather_fusion = bf16[128,128,128]{2,1,0:T(8,128)(2,1)} fusion(bf16[512,128,128]{2,1,0:T(8,128)(2,1)} %get-tuple-element.416, s32[1024]{0:T(1024)S(1)} %pad_clamp_fusion.3), kind=kCustom, calls=%fused_computation.clone.clone.1 | custom fusion | bytes 8389120 | tf_op jit(solution)/shard_map/while/body/eval_jaxpr/gather | solution.py:75
  125.2 4.6 fusion.95
  138.3 8.8 %gather_fusion = bf16[128,128,128]{2,1,0:T(8,128)(2,1)} fusion(bf16[512,128,128]{2,1,0:T(8,128)(2,1)} %get-tuple-element.416, s32[1024]{0:T(1024)S(1)} %pad_clamp_fusion.3), kind=kCustom, calls=%fused_computation.clone.clone.1 | custom fusion | bytes 8389120 | tf_op jit(solution)/shard_map/while/body/eval_jaxpr/gather | solution.py:75
  147.1 4.6 fusion.95
  160.3 8.8 %gather_fusion = bf16[128,128,128]{2,1,0:T(8,128)(2,1)} fusion(bf16[512,128,128]{2,1,0:T(8,128)(2,1)} %get-tuple-element.416, s32[1024]{0:T(1024)S(1)} %pad_clamp_fusion.3), kind=kCustom, calls=%fused_computation.clone.clone.1 | custom fusion | bytes 8389120 | tf_op jit(solution)/shard_map/while/body/eval_jaxpr/gather | solution.py:75
  169.1 4.6 fusion.95
  182.3 8.8 %gather_fusion = bf16[128,128,128]{2,1,0:T(8,128)(2,1)} fusion(bf16[512,128,128]{2,1,0:T(8,128)(2,1)} %get-tuple-element.416, s32[1024]{0:T(1024)S(1)} %pad_clamp_fusion.3), kind=kCustom, calls=%fused_computation.clone.clone.1 | custom fusion | bytes 8389120 | tf_op jit(solution)/shard_map/while/body/eval_jaxpr/gather | solution.py:75
  191.0 4.6 fusion.95
  204.2 8.8 %gather_fusion = bf16[128,128,128]{2,1,0:T(8,128)(2,1)} fusion(bf16[512,128,128]{2,1,0:T(8,128)(2,1)} %get-tuple-element.416, s32[1024]{0:T(1024)S(1)} %pad_clamp_fusion.3), kind=kCustom, calls=%fused_computation.clone.clone.1 | custom fusion | bytes 8389120 | tf_op jit(solution)/shard_map/while/body/eval_jaxpr/gather | solution.py:75
  213.0 4.6 fusion.95
  226.3 8.8 %gather_fusion = bf16[128,128,128]{2,1,0:T(8,128)(2,1)} fusion(bf16[512,128,128]{2,1,0:T(8,128)(2,1)} %get-tuple-element.416, s32[1024]{0:T(1024)S(1)} %pad_clamp_fusion.3), kind=kCustom, calls=%fused_computation.clone.clone.1 | custom fusion | bytes 8389120 | tf_op jit(solution)/shard_map/while/body/eval_jaxpr/gather | solution.py:75
  235.0 4.6 fusion.95
  248.2 8.8 %gather_fusion = bf16[128,128,128]{2,1,0:T(8,128)(2,1)} fusion(bf16[512,128,128]{2,1,0:T(8,128)(2,1)} %get-tuple-element.416, s32[1024]{0:T(1024)S(1)} %pad_clamp_fusion.3), kind=kCustom, calls=%fused_computation.clone.clone.1 | custom fusion | bytes 8389120 | tf_op jit(solution)/shard_map/while/body/eval_jaxpr/gather | solution.py:75
  257.0 4.6 fusion.95
  270.2 8.8 %gather_fusion = bf16[128,128,128]{2,1,0:T(8,128)(2,1)} fusion(bf16[512,128,128]{2,1,0:T(8,128)(2,1)} %get-tuple-element.416, s32[1024]{0:T(1024)S(1)} %pad_clamp_fusion.3), kind=kCustom, calls=%fused_computation.clone.clone.1 | custom fusion | bytes 8389120 | tf_op jit(solution)/shard_map/while/body/eval_jaxpr/gather | solution.py:75
  279.0 4.6 fusion.95
  292.2 8.8 %gather_fusion = bf16[128,128,128]{2,1,0:T(8,128)(2,1)} fusion(bf16[512,128,128]{2,1,0:T(8,128)(2,1)} %get-tuple-element.416, s32[1024]{0:T(1024)S(1)} %pad_clamp_fusion.3), kind=kCustom, calls=%fused_computation.clone.clone.1 | custom fusion | bytes 8389120 | tf_op jit(solution)/shard_map/while/body/eval_jaxpr/gather | solution.py:75
  300.9 4.6 fusion.95
  314.1 8.8 %gather_fusion = bf16[128,128,128]{2,1,0:T(8,128)(2,1)} fusion(bf16[512,128,128]{2,1,0:T(8,128)(2,1)} %get-tuple-element.416, s32[1024]{0:T(1024)S(1)} %pad_clamp_fusion.3), kind=kCustom, calls=%fused_computation.clone.clone.1 | custom fusion | bytes 8389120 | tf_op jit(solution)/shard_map/while/body/eval_jaxpr/gather | solution.py:75
  322.9 4.6 fusion.95
  336.1 8.8 %gather_fusion = bf16[128,128,128]{2,1,0:T(8,128)(2,1)} fusion(bf16[512,128,128]{2,1,0:T(8,128)(2,1)} %get-tuple-element.416, s32[1024]{0:T(1024)S(1)} %pad_clamp_fusion.3), kind=kCustom, calls=%fused_computation.clone.clone.1 | custom fusion | bytes 8389120 | tf_op jit(solution)/shard_map/while/body/eval_jaxpr/gather | solution.py:75
  344.9 4.6 fusion.95
  358.0 8.8 %gather_fusion = bf16[128,128,128]{2,1,0:T(8,128)(2,1)} fusion(bf16[512,128,128]{2,1,0:T(8,128)(2,1)} %get-tuple-element.416, s32[1024]{0:T(1024)S(1)} %pad_clamp_fusion.3), kind=kCustom, calls=%fused_computation.clone.clone.1 | custom fusion | bytes 8389120 | tf_op jit(solution)/shard_map/while/body/eval_jaxpr/gather | solution.py:75
  366.8 4.6 fusion.95
  380.0 8.8 %gather_fusion = bf16[128,128,128]{2,1,0:T(8,128)(2,1)} fusion(bf16[512,128,128]{2,1,0:T(8,128)(2,1)} %get-tuple-element.416, s32[1024]{0:T(1024)S(1)} %pad_clamp_fusion.3), kind=kCustom, calls=%fused_computation.clone.clone.1 | custom fusion | bytes 8389120 | tf_op jit(solution)/shard_map/while/body/eval_jaxpr/gather | solution.py:75
  388.8 4.6 fusion.95
  402.0 8.8 %gather_fusion = bf16[128,128,128]{2,1,0:T(8,128)(2,1)} fusion(bf16[512,128,128]{2,1,0:T(8,128)(2,1)} %get-tuple-element.416, s32[1024]{0:T(1024)S(1)} %pad_clamp_fusion.3), kind=kCustom, calls=%fused_computation.clone.clone.1 | custom fusion | bytes 8389120 | tf_op jit(solution)/shard_map/while/body/eval_jaxpr/gather | solution.py:75
  410.8 4.6 fusion.95
  424.0 8.8 %gather_fusion = bf16[128,128,128]{2,1,0:T(8,128)(2,1)} fusion(bf16[512,128,128]{2,1,0:T(8,128)(2,1)} %get-tuple-element.416, s32[1024]{0:T(1024)S(1)} %pad_clamp_fusion.3), kind=kCustom, calls=%fused_computation.clone.clone.1 | custom fusion | bytes 8389120 | tf_op jit(solution)/shard_map/while/body/eval_jaxpr/gather | solution.py:75
  432.7 4.6 fusion.95
  445.9 8.8 %gather_fusion = bf16[128,128,128]{2,1,0:T(8,128)(2,1)} fusion(bf16[512,128,128]{2,1,0:T(8,128)(2,1)} %get-tuple-element.416, s32[1024]{0:T(1024)S(1)} %pad_clamp_fusion.3), kind=kCustom, calls=%fused_computation.clone.clone.1 | custom fusion | bytes 8389120 | tf_op jit(solution)/shard_map/while/body/eval_jaxpr/gather | solution.py:75
  454.7 4.6 fusion.95
  470.0 7.4 %all-to-all-done.2 = f32[16,1,128]{2,1,0:T(1,128)S(1)} async-done(((f32[16,1,128]{2,1,0:T(1,128)}), f32[16,1,128]{2,1,0:T(1,128)S(1)}, u32[]{:S(2)}, u32[]{:S(2)}) %all-to-all-start.2) | async-done | bytes 8224 | tf_op jit(solution)/shard_map/all_to_all | solution.py:85
  477.4 5.0 fusion.39
  487.7 4.2 fusion.49
  497.1 29.6 %while.47 = (s32[]{:T(128)}, f32[8,16,32,128]{3,2,1,0:T(8,128)}, f32[8,16,24]{2,1,0:T(8,128)S(1)}, bf16[8,16,24,32,128]{4,3,2,1,0:T(8,128)(2,1)}, bf16[24,128,128]{2,1,0:T(8,128)(2,1)S(1)}, /*index=5*/s32[]{:T(128)}) while((s32[]{:T(128)}, f32[8,16,32,128]{3,2,1,0:T(8,128)}, f32[8,16,24]{2,1,0:T(8,128)S(1)}, ...), condition=%wide.region_21.22_spmd, body=%wide.region_19.21_spmd.sunk | while | flops 405733376 | bytes 4727369 | solution.py:139
  526.8 71.8 %while.49 = (s32[]{:T(128)}, f32[16,16,4096]{2,1,0:T(8,128)}, s32[16,128]{1,0:T(8,128)S(1)}, f32[16,128]{1,0:T(8,128)S(1)}, f32[16,128,32,128]{3,2,1,0:T(8,128)}, /*index=5*/s32[]{:T(128)}) while((s32[]{:T(128)}, f32[16,16,4096]{2,1,0:T(8,128)}, s32[16,128]{1,0:T(8,128)S(1)}, f32[16,128]{1,0:T(8,128)S(1)}, ...), condition=%wide.region_17.18_spmd.clone, body=%wide.region_16.17_spmd.clone.sunk | while | flops 101189632 | bytes 6557265 | solution.py:121
  598.6 4.9 copy.39
  603.5 78.9 %reduce-scatter.3.cloned.1.call-done = f32[16,32,128]{2,1,0:T(8,128)} async-done(((f32[256,32,128]{2,1,0:T(8,128)}), f32[16,32,128]{2,1,0:T(8,128)}) %reduce-scatter.3.cloned.1.call-update) | async-done | bytes 262160 | tf_op jit(solution)/shard_map/reduce_scatter | solution.py:122
  682.4 4.6 fusion.48
  (472 shorter events, 323.1 us)
Async XLA Ops:
  7.2 31.3 %all-gather.5.cloned.1.call-start = ((), (), s32[]{:S(2)}) async-start(), calls=%async_computation.9 | async-start | bytes 1179648 | tf_op jit(solution)/shard_map/all_gather | solution.py:90
  21.9 68.0 %all-to-all-start = ((s32[16,1,128]{2,1,0:T(1,128)}), s32[16,1,128]{2,1,0:T(1,128)S(1)}, u32[]{:S(2)}, u32[]{:S(2)}) async-start(s32[16,1,128]{2,1,0:T(1,128)} %get-tuple-element.239), calls=%async_computation | async-start | bytes 16384 | tf_op jit(solution)/shard_map/all_to_all | solution.py:64
  30.0 78.2 %all-gather.3.cloned.1.call-start = ((), (), s32[]{:S(2)}) async-start(), calls=%async_computation.8 | async-start | bytes 2228224 | tf_op jit(solution)/shard_map/all_gather | solution.py:67
  38.5 55.6 %copy-start.4 = (f32[16,64]{1,0:T(8,128)S(1)}, f32[16,64]{1,0:T(8,128)}, u32[]{:S(2)}) copy-start(f32[16,64]{1,0:T(8,128)} %param.19) | copy-start | bytes 12292
  89.8 9.6 %all-to-all-start.3 = ((f32[8,1,384]{2,1,0:T(1,128)}), f32[8,1,384]{2,1,0:T(1,128)S(1)}, u32[]{:S(2)}, u32[]{:S(2)}) async-start(f32[8,1,384]{2,1,0:T(1,128)} %reshape.347), calls=%async_computation.3 | async-start | bytes 24576 | tf_op jit(solution)/shard_map/all_to_all | solution.py:98
  99.5 14.8 %all-to-all-start.1 = ((s32[16,1,128]{2,1,0:T(1,128)}), s32[16,1,128]{2,1,0:T(1,128)S(1)}, u32[]{:S(2)}, u32[]{:S(2)}) async-start(s32[16,1,128]{2,1,0:T(1,128)} %get-tuple-element.238), calls=%async_computation.1 | async-start | bytes 16384 | tf_op jit(solution)/shard_map/all_to_all | solution.py:65
  125.2 4.6 copy-start
  132.1 4.1 copy-start.2
  147.1 4.6 copy-start
  154.1 4.0 copy-start.2
  169.1 4.6 copy-start
  176.1 4.1 copy-start.2
  180.1 1.3 copy-start.1
  191.0 4.6 copy-start
  198.0 4.1 copy-start.2
  213.0 4.6 copy-start
  220.0 4.1 copy-start.2
  224.1 1.3 copy-start.1
  235.0 4.6 copy-start
  242.0 4.0 copy-start.2
  257.0 4.6 copy-start
  264.0 4.1 copy-start.2
  279.0 4.6 copy-start
  286.0 4.1 copy-start.2
  300.9 4.6 copy-start
  307.9 4.1 copy-start.2
  312.0 1.3 copy-start.1
  322.9 4.6 copy-start
  329.9 4.0 copy-start.2
  344.9 4.6 copy-start
  351.8 4.1 copy-start.2
  366.8 4.6 copy-start
  373.8 4.1 copy-start.2
  388.8 4.6 copy-start
  395.8 4.1 copy-start.2
  410.8 4.6 copy-start
  417.8 4.0 copy-start.2
  421.9 1.3 copy-start.1
  432.7 4.6 copy-start
  439.7 4.1 copy-start.2
  454.7 4.6 copy-start
  461.7 4.1 copy-start.2
  465.8 11.6 %all-to-all-start.2 = ((f32[16,1,128]{2,1,0:T(1,128)}), f32[16,1,128]{2,1,0:T(1,128)S(1)}, u32[]{:S(2)}, u32[]{:S(2)}) async-start(f32[16,1,128]{2,1,0:T(1,128)} %bitcast.23), calls=%async_computation.2 | async-start | bytes 16384 | tf_op jit(solution)/shard_map/all_to_all | solution.py:85
  484.2 8.6 %all-to-all-start.5 = ((f32[8,1,384]{2,1,0:T(1,128)}), f32[8,1,384]{2,1,0:T(1,128)S(1)}, u32[]{:S(2)}, u32[]{:S(2)}) async-start(f32[8,1,384]{2,1,0:T(1,128)} %reshape.349), calls=%async_computation.6 | async-start | bytes 24576 | tf_op jit(solution)/shard_map/all_to_all | solution.py:129
  492.8 34.0 %all-to-all-start.4 = ((f32[16,1,128]{2,1,0:T(1,128)}), f32[16,1,128]{2,1,0:T(1,128)S(1)}, u32[]{:S(2)}, u32[]{:S(2)}) async-start(f32[16,1,128]{2,1,0:T(1,128)} %fusion.49), calls=%async_computation.4 | async-start | bytes 16384 | tf_op jit(solution)/shard_map/all_to_all | solution.py:110
  496.2 107.3 %reduce-scatter.5.cloned.1.call-start = ((), (), s32[]{:S(2)}) async-start(), calls=%async_computation.11 | async-start | bytes 2359296 | tf_op jit(solution)/shard_map/reduce_scatter | solution.py:140
  526.7 155.7 %reduce-scatter.3.cloned.1.call-start = ((), (), s32[]{:S(2)}) async-start(), calls=%async_computation.10 | async-start | bytes 4456448 | tf_op jit(solution)/shard_map/reduce_scatter | solution.py:122
  603.5 79.0 %copy-start.3 = (bf16[16,32,128]{2,1,0:T(8,128)(2,1)S(1)}, bf16[16,32,128]{2,1,0:T(8,128)(2,1)}, u32[]{:S(2)}) copy-start(bf16[16,32,128]{2,1,0:T(8,128)(2,1)} %param.14) | copy-start | bytes 393220
  (12 other events, 16.1 us)
Sparse Core Ops, SparseCore 0:
  10.3 25.7 all-gather.4
  38.8 45.1 all-gather.2
  526.8 34.3 reduce-scatter.4
  603.6 78.7 reduce-scatter.2
where the time goes:
time: 696 us; the launch traced here: 694 us
  local copies, waits for them, and re-layouts  240 us (34%)
  matrix products  188 us (27%)
  other arithmetic  122 us (18%)
  waiting for transfers between devices  96.4 us (14%)
  starting transfers between devices  30.8 us (4%)
  between operations  14 us (2%)
    gather x16, local copies, waits for them, and re-layouts, owner_weights(): tiles = index[passages]  141 us
    reduce_scatter x1, waiting for transfers between devices, on_device(): lax.psum_scatter(pieces.reshape((query_count * lax.axis_size('corpus'),)...  78.9 us
    dot_general x17, other arithmetic, tile_inverse(): jnp.einsum('pjd,pjd->pj', tiles, tiles, preferred_element_type=jnp.float32)  73.6 us
    dot_general x16, matrix products, add_source(): jnp.dot(select, terms, precision=highest, preferred_element_type=jnp.floa...  42.8 us
    dot_general x16, matrix products, owner_full(): jnp.einsum('pij,pjd->pid', weights, tiles, preferred_element_type=jnp.flo...  42.3 us
    dot_general x16, matrix products, pair_forward(): jnp.einsum('pid,pjd->pij', query_tiles, passage_tiles, preferred_element_...  38 us
    dynamic_slice x16, local copies, waits for them, and re-layouts, on_device(): pieces = lax.map(add_source, (owner_back, grad_part, got_query))  28.4 us
    dynamic_update_slice x16, other arithmetic, on_device(): tour_score, tour_weights = lax.map(neg_group, grouped)  26.8 us
  transfers between devices with their start and end apart: 10, of which 5 were waited for; matrix products, arithmetic and copies ran while one was open for 27% of the time, Pallas kernels for 0%

commit v1 on v0

v1 whole, which is shorter than its diff:
```python
import functools
import math

import jax
import jax.numpy as jnp
from jax import lax
from jax.experimental import pallas as pl
from jax.experimental.pallas import tpu as pltpu
from jax.sharding import PartitionSpec as P

MESH = pl.DeviceIdType.MESH
F32, BF16, I32 = jnp.float32, jnp.bfloat16, jnp.int32
EPS = 1e-6
SCALE = 10.0 * math.log2(math.e)
LN2 = math.log(2.0)
ROWS_NT = (((1,), (1,)), ((), ()))


def lane_sum_of_groups(x, group, lane, width):
    shift = group // 2
    while shift:
        x = x + jnp.where(
            (lane & shift) != 0, pltpu.roll(x, shift, 1), pltpu.roll(x, width - shift, 1)
        )
        shift //= 2
    return x


def transpose_pass(first, count, unroll, w_ref, inv_ref, tt_ref):
    def body(b, _):
        rows = [first + b * unroll + u for u in range(unroll)]
        wide = [jnp.transpose(w_ref[r]).astype(F32) for r in rows]
        inv = [lax.rsqrt(jnp.sum(x * x, axis=0, keepdims=True) + EPS) for x in wide]
        for u, r in enumerate(rows):
            inv_ref[pl.ds(r, 1)] = inv[u]
            tt_ref[r] = (wide[u] * (inv[u] * SCALE)).astype(BF16)
        return 0

    lax.fori_loop(0, count // unroll, body, 0)


def negatives(count, unroll, depth, rows_ref, w_ref, qt_ref, acc_ref, sum_ref):
    lane = lax.broadcasted_iota(I32, (1, 128), 1)
    groups = qt_ref.shape[1] // 128
    acc_ref[...] = jnp.zeros_like(acc_ref)
    sum_ref[...] = jnp.zeros_like(sum_ref)

    def body(b, _):
        tiles, flipped = [], []
        for u in range(unroll):
            wide = w_ref[rows_ref[b * unroll + u]].astype(F32)
            square = jnp.sum(wide * wide, axis=-1, keepdims=True)
            tiles.append((wide * (lax.rsqrt(square + EPS) * SCALE)).astype(BF16))
        for u in range(unroll):
            flipped.append(jnp.transpose(tiles[u]))
        items = [(g, u) for g in range(groups) for u in range(unroll)]
        n = len(items)
        sims, factor, expo, back = {}, {}, {}, {}
        total = sums = None
        for step in range(n + 3 * depth):
            i = step
            if i < n:
                g, u = items[i]
                sims[i] = jnp.dot(
                    tiles[u], qt_ref[:, g * 128 : (g + 1) * 128], preferred_element_type=F32
                )
            i = step - depth
            if 0 <= i < n:
                g, u = items[i]
                e = jnp.exp2(sims[i])
                logs = jnp.log2(jnp.sum(e, axis=0, keepdims=True))
                back[i] = jnp.dot(flipped[u], e.astype(BF16), preferred_element_type=F32)
                expo[i] = jnp.exp2(lane_sum_of_groups(logs, 32, lane, 128) * 0.1)
                factor[i] = expo[i] * jnp.exp2(-logs)
            i = step - 3 * depth
            if 0 <= i < n:
                g, u = items[i]
                here = back[i] * factor[i]
                total = here if u == 0 else total + here
                sums = expo[i] if u == 0 else sums + expo[i]
                if u == unroll - 1:
                    acc_ref[:, g * 128 : (g + 1) * 128] += total
                    sum_ref[0:1, g * 128 : (g + 1) * 128] += sums
        return 0

    lax.fori_loop(0, count // unroll, body, 0)


def listed(src, room, unroll, code, targ, keep, w_ref, inv_ref, tt_ref, q_ref, pa, pb, p1, p2):
    zero = jnp.zeros((32, 128), F32)
    one = jnp.zeros((1, 1), F32)

    def body(b, carry):
        acc_a, acc_b, acc_1, acc_2 = carry
        ks = [b * unroll + u for u in range(unroll)]
        cs = [code[src, k] for k in ks]
        sims = [
            jnp.dot(q_ref[c & 15], tt_ref[c >> 4], preferred_element_type=F32) for c in cs
        ]
        expo = [jnp.exp2(x) for x in sims]
        totals = [jnp.sum(x, axis=-1, keepdims=True) for x in expo]
        weights = [(x * inv_ref[pl.ds(c >> 4, 1)]).astype(BF16) for x, c in zip(expo, cs)]
        back = [
            jnp.dot(x, w_ref[c >> 4], preferred_element_type=F32) for x, c in zip(weights, cs)
        ]
        logs = [jnp.log2(x) for x in totals]
        score = [jnp.sum(x, axis=0, keepdims=True) * 0.1 for x in logs]
        top = [jnp.exp2(x) for x in score]
        flat = [jnp.exp2(-x) for x in logs]
        for u, k in enumerate(ks):
            here = back[u] * flat[u]
            stay, target = keep[src, k], targ[src, k]
            acc_a = acc_a * stay + here * top[u]
            acc_b = acc_b * stay + here * target
            acc_1 = acc_1 * stay + top[u]
            acc_2 = acc_2 * stay + score[u] * target
            pa[k] = acc_a
            pb[k] = acc_b
            p1[pl.ds(k, 1)] = jnp.broadcast_to(acc_1, (1, 128))
            p2[pl.ds(k, 1)] = jnp.broadcast_to(acc_2, (1, 128))
        return acc_a, acc_b, acc_1, acc_2

    lax.fori_loop(0, room // unroll, body, (zero, zero, one, one))


def kernel(
    owners, room, chunks,
    code, targ, keep, last, rows, q_ref, index_ref,
    grad_ref, s_ref,
    w, tt, inv, qall, qcur, qt, pa, pb, p1, p2, acc, nsum, back_buf, sum_buf, got, got_sum,
    load_sem, q_send, q_recv, b_send, b_recv, s_send, s_recv,
):
    me = lax.axis_index("corpus")
    count, tokens = qcur.shape[0], qcur.shape[1]

    barrier = pltpu.get_barrier_semaphore()

    def loads(j):
        part = pl.ds(j * (w.shape[0] // chunks), w.shape[0] // chunks)
        return pltpu.make_async_copy(index_ref.at[part], w.at[part], load_sem.at[j])

    def start_load(j, _):
        loads(j).start()
        return 0

    lax.fori_loop(0, chunks, start_load, 0)

    def greet(k, _):
        pl.semaphore_signal(
            barrier, inc=1, device_id={"corpus": lax.rem(me + k, owners)}, device_id_type=MESH
        )
        return 0

    lax.fori_loop(1, owners, greet, 0)

    wide = q_ref[...].astype(F32)
    radius = jnp.sqrt(jnp.sum(wide * wide, axis=-1, keepdims=True) + EPS)
    rounded = (wide / radius).astype(BF16)
    qcur[...] = rounded.reshape(qcur.shape)
    qall[me] = rounded.reshape(qcur.shape)
    qt[...] = jnp.transpose(rounded)

    pl.semaphore_wait(barrier, owners - 1)

    def q_copy(k):
        return pltpu.make_async_remote_copy(
            src_ref=qcur,
            dst_ref=qall.at[me],
            send_sem=q_send.at[k],
            recv_sem=q_recv.at[k],
            device_id={"corpus": lax.rem(me + k, owners)},
            device_id_type=MESH,
        )

    def q_start(k, _):
        q_copy(k).start()
        return 0

    lax.fori_loop(1, owners, q_start, 0)

    part = w.shape[0] // chunks

    def prepare(j, _):
        loads(j).wait()
        transpose_pass(j * part, part, 4, w, inv, tt)
        return 0

    lax.fori_loop(0, chunks, prepare, 0)
    negatives(rows.shape[0], 2, 2, rows, w, qt, acc, nsum)

    def q_sent(k, _):
        q_copy(k).wait_send()
        return 0

    lax.fori_loop(1, owners, q_sent, 0)

    zero = jnp.zeros((32, 128), F32)
    pa[room] = zero
    pb[room] = zero
    p1[room : room + 8] = jnp.zeros((8, 128), F32)
    p2[room : room + 8] = jnp.zeros((8, 128), F32)

    def back_copy(k, src):
        return (
            pltpu.make_async_remote_copy(
                src_ref=back_buf.at[k], dst_ref=got.at[k],
                send_sem=b_send.at[k], recv_sem=b_recv.at[k],
                device_id={"corpus": src}, device_id_type=MESH,
            ),
            pltpu.make_async_remote_copy(
                src_ref=sum_buf.at[k], dst_ref=got_sum.at[k],
                send_sem=s_send.at[k], recv_sem=s_recv.at[k],
                device_id={"corpus": src}, device_id_type=MESH,
            ),
        )

    def source(k, _):
        src = lax.rem(me + owners - k, owners)

        @pl.when(k > 0)
        def _():
            q_copy(k).wait_recv()

        qcur[...] = qall[src]
        listed(src, room, 16, code, targ, keep, w, inv, tt, qcur, pa, pb, p1, p2)

        def extract(q, _):
            at = last[src, q]
            back_buf[k, q, 0:tokens] = pa[at].astype(BF16)
            back_buf[k, q, tokens : 2 * tokens] = pb[at].astype(BF16)
            sum_buf[k, 0, pl.ds(q, 1)] = p1[pl.ds(at, 1)]
            sum_buf[k, 1, pl.ds(q, 1)] = p2[pl.ds(at, 1)]
            return 0

        lax.fori_loop(0, count, extract, 0, unroll=4)

        @pl.when(k > 0)
        def _():
            for copy in back_copy(k, src):
                copy.start()

        return 0

    lax.fori_loop(0, owners, source, 0)

    def take(k, _):
        for copy in back_copy(k, lax.rem(me + owners - k, owners)):
            copy.wait()
        return 0

    lax.fori_loop(1, owners, take, 0)

    sums = sum_buf[0]
    for k in range(1, owners):
        sums = sums + got_sum[k]
    p1[0:count] = sums[0]
    p2[0:count] = sums[1]
    pa_flat = jnp.transpose(acc[...]) * (1.0 / SCALE)
    tn = jnp.transpose(jnp.broadcast_to(nsum[0:1], (128, count * tokens)))
    for q in range(count):
        pa[q] = pa_flat[q * tokens : (q + 1) * tokens]
        pb[q] = tn[q * tokens : (q + 1) * tokens]

    def finish(q, _):
        part_a = pa[q] + back_buf[0, q, 0:tokens].astype(F32)
        part_b = back_buf[0, q, tokens : 2 * tokens].astype(F32)
        for k in range(1, owners):
            part_a = part_a + got[k, q, 0:tokens].astype(F32)
            part_b = part_b + got[k, q, tokens : 2 * tokens].astype(F32)
        whole = pb[q] + p1[pl.ds(q, 1)]
        pulled = part_a / whole - part_b
        own = q_ref[pl.ds(pl.multiple_of(q * tokens, tokens), tokens)].astype(F32)
        rad = jnp.sqrt(jnp.sum(own * own, axis=-1, keepdims=True) + EPS)
        unit = own / rad
        along = jnp.sum(unit * pulled, axis=-1, keepdims=True)
        grad_ref[q] = (pulled - unit * along) / rad
        s_ref[0, pl.ds(q, 1)] = whole[0:1]
        s_ref[1, pl.ds(q, 1)] = p2[pl.ds(q, 1)]
        return 0

    lax.fori_loop(0, count, finish, 0)


def step(queries, index, cand_owner, cand_row, neg_row, teacher):
    count, tokens, dim = queries.shape
    listed_count = cand_row.shape[1]
    owners = lax.axis_size("corpus")
    pairs = count * listed_count
    room = 2 * pairs // owners
    passages = index.shape[0]

    log_target = teacher - jnp.log(jnp.sum(jnp.exp(teacher), axis=1, keepdims=True))
    target = jnp.exp(log_target)

    names = cand_owner.reshape(-1)
    hits = names[:, None] == jnp.arange(owners, dtype=I32)[None, :]
    order = jnp.arange(pairs, dtype=I32)
    before = (order[None, :] < order[:, None]).astype(BF16)
    ranks = jnp.dot(before, hits.astype(BF16), preferred_element_type=F32)
    slots = jnp.sum(jnp.where(hits, ranks, 0.0), axis=1).astype(I32)
    places = names * room + slots
    placer = (places[:, None] == jnp.arange(owners * room, dtype=I32)[None, :]).astype(F32)
    codes = cand_row.reshape(-1) * count + order // listed_count
    values = jnp.stack([codes.astype(F32), target.reshape(-1)], axis=0)
    placed = jnp.dot(
        values, placer, precision=lax.Precision.HIGHEST, preferred_element_type=F32
    ).reshape(2, owners, room)
    number = jnp.sum(hits.reshape(count, listed_count, owners).astype(I32), axis=1).T
    upto = jnp.sum(
        jnp.where(jnp.arange(count)[:, None] <= jnp.arange(count)[None, :], number[:, :, None], 0),
        axis=1,
    )
    ends = jnp.where(number > 0, upto - 1, room).astype(F32)
    ends = jnp.pad(ends, ((0, 0), (0, room - count)))
    message = jnp.concatenate([placed[0], placed[1], ends], axis=1)[:, None, :]
    message = lax.all_to_all(message, "corpus", split_axis=0, concat_axis=0, tiled=True)[:, 0]
    code = message[:, :room].astype(I32)
    targ = message[:, room : 2 * room]
    last = message[:, 2 * room : 2 * room + count].astype(I32)
    whose = code % count
    keep = jnp.concatenate(
        [jnp.zeros((owners, 1), F32), (whose[:, 1:] == whose[:, :-1]).astype(F32)], axis=1
    )
    rows = lax.all_gather(neg_row.reshape(-1), "blk", axis=0, tiled=True)

    smem = pl.BlockSpec(memory_space=pltpu.SMEM)
    vmem = pl.BlockSpec(memory_space=pltpu.VMEM)
    dma = pltpu.SemaphoreType.DMA
    chunks = 16
    grads, sums = pl.pallas_call(
        functools.partial(kernel, owners, room, chunks),
        out_shape=[
            jax.ShapeDtypeStruct((count, tokens, dim), F32),
            jax.ShapeDtypeStruct((2, count, 128), F32),
        ],
        in_specs=[smem] * 5 + [vmem, pl.BlockSpec(memory_space=pl.ANY)],
        out_specs=[vmem, vmem],
        scratch_shapes=[
            pltpu.VMEM(index.shape, BF16),
            pltpu.VMEM((passages, dim, index.shape[1]), BF16),
            pltpu.VMEM((passages, 128), F32),
            pltpu.VMEM((owners, count, tokens, dim), BF16),
            pltpu.VMEM((count, tokens, dim), BF16),
            pltpu.VMEM((dim, count * tokens), BF16),
            pltpu.VMEM((room + 1, tokens, dim), F32),
            pltpu.VMEM((room + 1, tokens, dim), F32),
            pltpu.VMEM((room + 8, 128), F32),
            pltpu.VMEM((room + 8, 128), F32),
            pltpu.VMEM((dim, count * tokens), F32),
            pltpu.VMEM((8, count * tokens), F32),
            pltpu.VMEM((owners, count, 2 * tokens, dim), BF16),
            pltpu.VMEM((owners, 2, count, 128), F32),
            pltpu.VMEM((owners, count, 2 * tokens, dim), BF16),
            pltpu.VMEM((owners, 2, count, 128), F32),
            dma((chunks,)), dma((owners,)), dma((owners,)), dma((owners,)), dma((owners,)),
            dma((owners,)), dma((owners,)),
        ],
        compiler_params=pltpu.CompilerParams(
            collective_id=0, has_side_effects=True, vmem_limit_bytes=58 << 20
        ),
        name="distill",
    )(code, targ, keep, last, rows, queries.reshape(count * tokens, dim), index)

    spread = jnp.log(sums[0, :, 0])
    losses = (
        jnp.sum(target * log_target, axis=1)
        - LN2 * sums[1, :, 0]
        + spread * jnp.sum(target, axis=1)
    )
    return losses, grads


def solution(mesh):
    both = ("corpus", "blk")
    return jax.shard_map(
        step,
        mesh=mesh,
        in_specs=(
            P(both, None, None), P("corpus", None, None), P(both, None, None),
            P(both, None), P(both, None), P(both, None),
        ),
        out_specs=(P(both), P(both, None, None)),
        check_vma=False,
    )
```

time: 696 us -> 217 us (0.31)
  local copies, waits for them, and re-layouts: 240 us -> 5.28 us
  matrix products: 188 us -> 3.27 us
  Pallas kernels: 0 us -> 180 us
  other arithmetic: 122 us -> 8.29 us
  waiting for transfers between devices: 96.4 us -> 0.01 us
  starting transfers between devices: 30.8 us -> 8.13 us
  between operations: 14 us -> 1.37 us
  blocking collectives: 0 us -> 9.8 us
    dot_general x83 -> x2, matrix products: 188 us -> 3.27 us  [the longest x1 2.77 us: step(): jnp.dot(values, placer, precision=lax.Precision.HIGHEST, preferred_elemen...]
    pallas_call x0 -> x1, Pallas kernels: none -> 180 us  [step(): pl.pallas_call(functools.partial(kernel, owners, room, chunks), out_shape...]
    gather x17 -> x0, local copies, waits for them, and re-layouts: 147 us -> none  [the longest x16 141 us: owner_weights(): tiles = index[passages]]
    reduce_scatter x2 -> x0, waiting for transfers between devices: 78.9 us -> none  [the longest x1 78.9 us: on_device(): lax.psum_scatter(pieces.reshape((query_count * lax.axis_size('corpus'),)...]
    dot_general x17 -> x0, other arithmetic: 73.6 us -> none  [tile_inverse(): jnp.einsum('pjd,pjd->pj', tiles, tiles, preferred_element_type=jnp.float32)]
    dynamic_slice x32 -> x0, local copies, waits for them, and re-layouts: 29 us -> none  [the longest x16 28.4 us: on_device(): pieces = lax.map(add_source, (owner_back, grad_part, got_query))]
    dynamic_update_slice x16 -> x0, other arithmetic: 26.8 us -> none  [on_device(): tour_score, tour_weights = lax.map(neg_group, grouped)]
    dynamic_update_slice x24 -> x0, local copies, waits for them, and re-layouts: 26.6 us -> none  [the longest x16 20.7 us: on_device(): lax.map(owner_full, (copy_groups, got_query, got_row))]
  transfers between devices with their start and end apart: 10 -> 1, of which waited for: 5 -> 0; matrix products, arithmetic and copies ran while one was open for 27% -> 1% of each run, Pallas kernels for 0% -> 0%
where the time goes in v1:
time: 217 us; the launch traced here: 216 us
  Pallas kernels  180 us (83%)
  blocking collectives  9.8 us (5%)
  other arithmetic  8.29 us (4%)
  starting transfers between devices  8.13 us (4%)
  local copies, waits for them, and re-layouts  5.28 us (2%)
  matrix products  3.27 us (2%)
    pallas_call x1, Pallas kernels, step(): pl.pallas_call(functools.partial(kernel, owners, room, chunks), out_shape...  180 us
    all_gather x1, blocking collectives, step(): rows = lax.all_gather(neg_row.reshape(-1), 'blk', axis=0, tiled=True)  9.8 us
    all_to_all x1, starting transfers between devices, step(): lax.all_to_all(message, 'corpus', split_axis=0, concat_axis=0, tiled=True)  8.13 us
  transfers between devices with their start and end apart: 1, of which 0 were waited for; matrix products, arithmetic and copies ran while one was open for 1% of the time, Pallas kernels for 0%

profile of v1, /device:TPU:0, one launch (start us, length us, event | category | flops | bytes accessed | tf_op | source)
XLA Modules:
  0.0 215.7 jit_solution(6607476103344156008)
XLA Ops:
  0.6 0.8 exponential_reduce_fusion
  1.5 0.5 broadcast.103
  2.0 1.4 reduce.7
  3.4 0.1 reshape.98
  3.4 0.5 fusion.4
  3.9 1.0 convert_reduce_fusion
  5.0 0.1 copy.13
  5.1 0.1 select_reduce_fusion
  5.2 0.1 copy.14
  5.3 0.1 copy.17
  5.3 0.7 broadcast_multiply_fusion
  6.0 0.1 mul.41
  6.1 0.9 multiply_reduce_fusion.1
  7.0 0.1 stack_reshape.3
  7.1 2.8 %fusion = f32[2,2048]{1,0:T(2,128)S(1)} fusion(s32[1024]{0:T(1024)S(1)} %convert_add_fusion, f32[1,1024]{1,0:T(1,128)S(1)} %stack_reshape.3, f32[1,1024]{1,0:T(1,128)S(1)} %fusion.11), kind=kOutput, calls=%fused_computation.1 | convolution fusion | flops 52430848 | bytes 28672 | tf_op jit(solution)/shard_map/dot_general | solution.py:305
  9.9 0.6 broadcast_in_dim.41
  10.5 8.1 %all-to-all-start = ((f32[16,1,384]{2,1,0:T(1,128)}), f32[16,1,384]{2,1,0:T(1,128)S(1)}, u32[]{:S(2)}, u32[]{:S(2)}) async-start(f32[16,1,384]{2,1,0:T(1,128)} %broadcast_in_dim.41), calls=%async_computation | async-start | bytes 49152 | tf_op jit(solution)/shard_map/all_to_all | solution.py:316
  18.7 1.2 dynamic-slice
  20.6 0.8 bitcast_dynamic-update-slice_fusion
  21.3 9.8 %all-reduce.2.rows = s32[192]{0:T(256)} all-reduce(s32[192]{0:T(256)S(1)} %bitcast_dynamic-update-slice_fusion), channel_id=2, replica_groups=mesh['corpus'=16,'blk'=8] {'blk'}, use_global_device_ids=true, to_apply=%add.2 | all-reduce | flops 192 | bytes 1536 | tf_op jit(solution)/shard_map/all_gather | solution.py:324
  31.1 0.0 all-to-all-done
  31.1 0.6 slice_convert_fusion.last
  31.8 0.6 fusion.14
  32.4 0.1 slice_compare_fusion
  32.4 0.7 pad_convert_fusion.keep
  33.1 179.6 %distill.1 = (f32[16,32,128]{2,1,0:T(8,128)}, f32[2,16,128]{2,1,0:T(8,128)}) custom-call(s32[16,128]{1,0:T(8,128)} %get-tuple-element.11.code, f32[16,128]{1,0:T(8,128)} %get-tuple-element.10.targ, f32[16,128]{1,0:T(8,128)} %pad_convert_fusion.keep, s32[16,16]{1,0:T(8,128)} %slice_convert_fusion.last, s32[192]{0:T(256)} %all-reduce.2.rows, ...), custom_call_target="tpu_custom_call" | custom-call | tf_op jit(solution)/shard_map/distill/pallas_call | solution.py:330
  212.7 0.8 multiply_reduce_fusion
  213.5 0.5 multiply_add_fusion
  214.0 1.7 copy.22
  (10 shorter events, 0.1 us)
Async XLA Ops:
  10.5 20.6 %all-to-all-start = ((f32[16,1,384]{2,1,0:T(1,128)}), f32[16,1,384]{2,1,0:T(1,128)S(1)}, u32[]{:S(2)}, u32[]{:S(2)}) async-start(f32[16,1,384]{2,1,0:T(1,128)} %broadcast_in_dim.41), calls=%async_computation | async-start | bytes 49152 | tf_op jit(solution)/shard_map/all_to_all | solution.py:316

commit v2 on v1

v2 whole, which is shorter than its diff:
```python
import functools
import math

import jax
import jax.numpy as jnp
from jax import lax
from jax.experimental import pallas as pl
from jax.experimental.pallas import tpu as pltpu
from jax.sharding import PartitionSpec as P

MESH = pl.DeviceIdType.MESH
F32, BF16, I32 = jnp.float32, jnp.bfloat16, jnp.int32
EPS = 1e-6
SCALE = 10.0 * math.log2(math.e)
LN2 = math.log(2.0)
ROWS_NT = (((1,), (1,)), ((), ()))


def lane_sum_of_groups(x, group, lane, width):
    shift = group // 2
    while shift:
        x = x + jnp.where(
            (lane & shift) != 0, pltpu.roll(x, shift, 1), pltpu.roll(x, width - shift, 1)
        )
        shift //= 2
    return x


def transpose_pass(first, count, unroll, w_ref, inv_ref, tt_ref):
    def body(b, _):
        rows = [first + b * unroll + u for u in range(unroll)]
        wide = [jnp.transpose(w_ref[r]).astype(F32) for r in rows]
        inv = [lax.rsqrt(jnp.sum(x * x, axis=0, keepdims=True) + EPS) for x in wide]
        for u, r in enumerate(rows):
            inv_ref[pl.ds(r, 1)] = inv[u]
            tt_ref[r] = (wide[u] * (inv[u] * SCALE)).astype(BF16)
        return 0

    lax.fori_loop(0, count // unroll, body, 0)


def build_tables(owners, room, codes_end, names_ref, row_ref, target, turned, place, codes, wants, ends, tab_i, tab_f):
    count, listed = row_ref.shape
    lane = lax.broadcasted_iota(I32, (128, 128), 1)
    line = lax.broadcasted_iota(I32, (128, 128), 0)
    lane_f = lane.astype(F32)
    lower = (lane < line).astype(F32).astype(BF16)

    def flip(x):
        turned[...] = jnp.zeros_like(turned)
        turned[0:count, 0:listed] = x
        return jnp.transpose(turned[...])

    number = lax.broadcasted_iota(I32, row_ref.shape, 0)
    names = flip(names_ref[...].astype(F32))
    code = flip((row_ref[...] * count + number).astype(F32))
    want = flip(target)
    per = 128 // listed
    blocks = count // per
    offset = jnp.zeros((1, 128), F32)
    ends[...] = jnp.zeros_like(ends)
    for r in range(blocks):
        def column(x):
            return jnp.concatenate(
                [x[0:listed, r * per + i : r * per + i + 1] for i in range(per)], axis=0
            )

        hit = (column(names) == lane_f)
        ones = hit.astype(F32)
        rank = jnp.dot(lower, ones.astype(BF16), preferred_element_type=F32) + offset
        where = jnp.sum(jnp.where(hit, rank + lane_f * room, 0.0), axis=1, keepdims=True)
        place[r] = jnp.broadcast_to(where, (128, 128))
        codes[r] = jnp.broadcast_to(column(code), (128, 128))
        wants[r] = jnp.broadcast_to(column(want), (128, 128))
        for i in range(per):
            at = (i + 1) * listed - 1
            upto = rank[at : at + 1] + ones[at : at + 1]
            start = offset if i == 0 else before
            ends[r * per + i : r * per + i + 1] = jnp.where(
                upto > start, jnp.minimum(upto - 1.0, float(room)), float(room)
            )
            before = upto
        offset = before
    turned[...] = jnp.transpose(ends[...])
    tab_i[...] = jnp.zeros_like(tab_i)
    tab_f[...] = jnp.zeros_like(tab_f)
    mark = lax.broadcasted_iota(I32, (1, 128), 1)

    def one_owner(o, _):
        slot = lane_f + (o * room).astype(F32)
        sum_c = jnp.zeros((128, 128), F32)
        sum_w = jnp.zeros((128, 128), F32)
        for r in range(blocks):
            here = place[r] == slot
            sum_c = sum_c + jnp.where(here, codes[r], 0.0)
            sum_w = sum_w + jnp.where(here, wants[r], 0.0)
        c = jnp.clip(jnp.sum(sum_c, axis=0, keepdims=True).astype(I32), 0, codes_end - 1)
        whose = c & (count - 1)
        same = (whose == pltpu.roll(whose, 1, 1)) & (mark > 0)
        tab_i[o, 0:1] = c
        tab_i[o, 1:2] = jnp.clip(turned[pl.ds(o, 1)].astype(I32), 0, room)
        tab_f[o, 0:1] = jnp.sum(sum_w, axis=0, keepdims=True)
        tab_f[o, 1:2] = jnp.where(same, 1.0, 0.0)
        return 0

    lax.fori_loop(0, owners, one_owner, 0)


def negatives(unroll, rows_ref, holders, each, tt_ref, qt_ref, acc_ref, sum_ref):
    width = qt_ref.shape[1]
    lane = lax.broadcasted_iota(I32, (1, width), 1)
    acc_ref[...] = jnp.zeros_like(acc_ref)
    sum_ref[...] = jnp.zeros_like(sum_ref)
    steps = each // unroll

    def body(b, _):
        holder, first = b // steps, lax.rem(b, steps) * unroll
        flipped = [tt_ref[rows_ref[holder, 0, first + u]] for u in range(unroll)]
        tiles = jnp.concatenate([jnp.transpose(t) for t in flipped], axis=0)
        sims = jnp.dot(tiles, qt_ref[...], preferred_element_type=F32)
        expo = jnp.exp2(sims)
        parts = [expo[u * 128 : (u + 1) * 128] for u in range(unroll)]
        logs = jnp.log2(
            jnp.concatenate([jnp.sum(x, axis=0, keepdims=True) for x in parts], axis=0)
        )
        top = jnp.exp2(lane_sum_of_groups(logs, 32, lane, width) * 0.1)
        factor = top * jnp.exp2(-logs)
        weights = jnp.concatenate(
            [(parts[u] * factor[u : u + 1]).astype(BF16) for u in range(unroll)], axis=0
        )
        acc_ref[...] += jnp.dot(
            jnp.concatenate(flipped, axis=1), weights, preferred_element_type=F32
        )
        sum_ref[0:1] += jnp.sum(top, axis=0, keepdims=True)
        return 0

    lax.fori_loop(0, holders * steps, body, 0)


def paired_dots(left, right):
    zero = jnp.zeros(left[0].shape, left[0].dtype)
    m = left[0].shape[0]
    out = []
    for i in range(0, len(left), 2):
        both = jnp.concatenate(
            [
                jnp.concatenate([left[i], zero], axis=1),
                jnp.concatenate([zero, left[i + 1]], axis=1),
            ],
            axis=0,
        )
        stacked = jnp.concatenate([right[i], right[i + 1]], axis=0)
        two = jnp.dot(both, stacked, preferred_element_type=F32)
        out += [two[:m], two[m:]]
    return out


def listed_pairs(src, room, unroll, tab_i, tab_f, w_ref, inv_ref, tt_ref, q_ref, pa, pb, p1, p2):
    zero = jnp.zeros((32, 128), F32)
    one = jnp.zeros((1, 1), F32)

    def body(b, carry):
        acc_a, acc_b, acc_1, acc_2 = carry
        ks = [b * unroll + u for u in range(unroll)]
        cs = [tab_i[src, 0, k] for k in ks]
        sims = paired_dots([q_ref[c & 15] for c in cs], [tt_ref[c >> 4] for c in cs])
        expo = [jnp.exp2(x) for x in sims]
        totals = [jnp.sum(x, axis=-1, keepdims=True) for x in expo]
        weights = [(x * inv_ref[pl.ds(c >> 4, 1)]).astype(BF16) for x, c in zip(expo, cs)]
        back = paired_dots(weights, [w_ref[c >> 4] for c in cs])
        logs = [jnp.log2(x) for x in totals]
        score = [jnp.sum(x, axis=0, keepdims=True) * 0.1 for x in logs]
        top = [jnp.exp2(x) for x in score]
        flat = [jnp.exp2(-x) for x in logs]
        for u, k in enumerate(ks):
            here = back[u] * flat[u]
            target, stay = tab_f[src, 0, k], tab_f[src, 1, k]
            acc_a = acc_a * stay + here * top[u]
            acc_b = acc_b * stay + here * target
            acc_1 = acc_1 * stay + top[u]
            acc_2 = acc_2 * stay + score[u] * target
            pa[k] = acc_a.astype(BF16)
            pb[k] = acc_b.astype(BF16)
            p1[pl.ds(k, 1)] = jnp.broadcast_to(acc_1, (1, 128))
            p2[pl.ds(k, 1)] = jnp.broadcast_to(acc_2, (1, 128))
        return acc_a, acc_b, acc_1, acc_2

    lax.fori_loop(0, room // unroll, body, (zero, zero, one, one))


def kernel(
    owners, holders, room, chunks, sampled,
    names_ref, row_ref, neg_ref, teacher_ref, q_ref, index_ref,
    grad_ref, loss_ref,
    w, tt, inv, qall, qcur, qt, pa, pb, p1, p2, acc, nsum, flat_a, flat_s, stats,
    turned, ends, place, codes, wants, tab_i, tab_f, all_i, all_f, all_n,
    back_buf, sum_buf, got, got_sum,
    code_s, mark_s, rows_s,
    load_sem, q_send, q_recv, i_send, i_recv, f_send, f_recv, n_send, n_recv,
    b_send, b_recv, s_send, s_recv, smem_sem,
):
    me = lax.axis_index("corpus")
    seat = lax.axis_index("blk")
    count, tokens = qcur.shape[0], qcur.shape[1]
    part = w.shape[0] // chunks
    barrier = pltpu.get_barrier_semaphore()

    def each(first, last, act):
        def body(k, _):
            act(k)
            return 0

        lax.fori_loop(first, last, body, 0)

    def loads(j):
        rows = pl.ds(j * part, part)
        return pltpu.make_async_copy(index_ref.at[rows], w.at[rows], load_sem.at[j])

    def owner(k):
        return {"corpus": lax.rem(me + k, owners)}

    def holder(k):
        return {"blk": lax.rem(seat + k, holders)}

    def remote(src, dst, send, recv, k, device):
        return pltpu.make_async_remote_copy(
            src_ref=src, dst_ref=dst, send_sem=send.at[k], recv_sem=recv.at[k],
            device_id=device, device_id_type=MESH,
        )

    def greet(device):
        pl.semaphore_signal(barrier, inc=1, device_id=device, device_id_type=MESH)

    each(0, chunks, lambda j: loads(j).start())
    each(1, owners, lambda k: greet(owner(k)))
    each(1, holders, lambda k: greet(holder(k)))

    wide = q_ref[...].astype(F32)
    radius = jnp.sqrt(jnp.sum(wide * wide, axis=-1, keepdims=True) + EPS)
    rounded = (wide / radius).astype(BF16)
    qcur[...] = rounded.reshape(qcur.shape)
    qall[me] = rounded.reshape(qcur.shape)
    qt[...] = jnp.transpose(rounded)
    all_n[seat] = neg_ref[...]

    pl.semaphore_wait(barrier, owners + holders - 2)

    def n_copy(k):
        return remote(neg_ref, all_n.at[seat], n_send, n_recv, k, holder(k))

    def q_copy(k):
        return remote(qcur, qall.at[me], q_send, q_recv, k, owner(k))

    def table_copies(k):
        to = lax.rem(me + k, owners)
        return (
            remote(tab_i.at[to], all_i.at[me], i_send, i_recv, k, owner(k)),
            remote(tab_f.at[to], all_f.at[me], f_send, f_recv, k, owner(k)),
        )

    each(1, holders, lambda k: n_copy(k).start())
    each(1, owners, lambda k: q_copy(k).start())

    teacher = teacher_ref[...]
    log_target = teacher - jnp.log(jnp.sum(jnp.exp(teacher), axis=1, keepdims=True))
    target = jnp.exp(log_target)
    stats[0] = jnp.broadcast_to(jnp.sum(target * log_target, axis=1, keepdims=True), (count, 128))
    stats[1] = jnp.broadcast_to(jnp.sum(target, axis=1, keepdims=True), (count, 128))
    build_tables(
        owners, room, w.shape[0] * count, names_ref, row_ref, target, turned, place, codes, wants, ends, tab_i, tab_f
    )
    all_i[me] = tab_i[me]
    all_f[me] = tab_f[me]
    each(1, owners, lambda k: [copy.start() for copy in table_copies(k)])

    def prepare(j):
        loads(j).wait()
        transpose_pass(j * part, part, 8, w, inv, tt)

    each(0, chunks, prepare)
    each(1, holders, lambda k: n_copy(k).wait())
    each(1, owners, lambda k: [copy.wait() for copy in table_copies(k)])
    moves = [
        pltpu.make_async_copy(all_n, rows_s, smem_sem.at[0]),
        pltpu.make_async_copy(all_i, code_s, smem_sem.at[1]),
        pltpu.make_async_copy(all_f, mark_s, smem_sem.at[2]),
    ]
    for move in moves:
        move.start()
    for move in moves:
        move.wait()
    negatives(8, rows_s, holders, sampled, tt, qt, acc, nsum)
    each(1, owners, lambda k: q_copy(k).wait_send())

    pa[room] = jnp.zeros((tokens, 128), BF16)
    pb[room] = jnp.zeros((tokens, 128), BF16)
    p1[room : room + 8] = jnp.zeros((8, 128), F32)
    p2[room : room + 8] = jnp.zeros((8, 128), F32)

    def back_copies(k):
        to = {"corpus": lax.rem(me + owners - k, owners)}
        return (
            remote(back_buf.at[k], got.at[k], b_send, b_recv, k, to),
            remote(sum_buf.at[k], got_sum.at[k], s_send, s_recv, k, to),
        )

    def source(k):
        src = lax.rem(me + owners - k, owners)

        @pl.when(k > 0)
        def _():
            q_copy(k).wait_recv()

        qcur[...] = qall[src]
        listed_pairs(src, room, 32, code_s, mark_s, w, inv, tt, qcur, pa, pb, p1, p2)

        def extract(q, _):
            at = code_s[src, 1, q]
            back_buf[k, q, 0:tokens] = pa[at]
            back_buf[k, q, tokens : 2 * tokens] = pb[at]
            sum_buf[k, 0, pl.ds(q, 1)] = p1[pl.ds(at, 1)]
            sum_buf[k, 1, pl.ds(q, 1)] = p2[pl.ds(at, 1)]
            return 0

        lax.fori_loop(0, count, extract, 0, unroll=4)

        @pl.when(k > 0)
        def _():
            for copy in back_copies(k):
                copy.start()

    each(0, owners, source)

    turned_a = jnp.transpose(acc[...]) * (1.0 / SCALE)
    turned_s = jnp.transpose(jnp.broadcast_to(nsum[0:1], (128, count * tokens)))
    flat_a[...] = turned_a.reshape(flat_a.shape)
    flat_s[...] = turned_s.reshape(flat_s.shape)

    each(1, owners, lambda k: [copy.wait() for copy in back_copies(k)])
    sums = sum_buf[0]
    for k in range(1, owners):
        sums = sums + got_sum[k]
    p1[0:count] = sums[0]
    p2[0:count] = sums[1]

    def finish(q, _):
        part_a = flat_a[q] + back_buf[0, q, 0:tokens].astype(F32)
        part_b = back_buf[0, q, tokens : 2 * tokens].astype(F32)
        for k in range(1, owners):
            part_a = part_a + got[k, q, 0:tokens].astype(F32)
            part_b = part_b + got[k, q, tokens : 2 * tokens].astype(F32)
        whole = flat_s[q] + p1[pl.ds(q, 1)]
        pulled = part_a / whole - part_b
        own = q_ref[pl.ds(pl.multiple_of(q * tokens, tokens), tokens)].astype(F32)
        rad = jnp.sqrt(jnp.sum(own * own, axis=-1, keepdims=True) + EPS)
        unit = own / rad
        along = jnp.sum(unit * pulled, axis=-1, keepdims=True)
        grad_ref[q] = (pulled - unit * along) / rad
        one = pl.ds(q, 1)
        loss_ref[one] = stats[0, one] - LN2 * p2[one] + jnp.log(whole[0:1]) * stats[1, one]
        return 0

    lax.fori_loop(0, count, finish, 0, unroll=2)


def step(queries, index, cand_owner, cand_row, neg_row, teacher):
    count, tokens, dim = queries.shape
    listed = cand_row.shape[1]
    owners, holders = lax.axis_size("corpus"), lax.axis_size("blk")
    room = 2 * count * listed // owners
    passages = index.shape[0]
    width = count * tokens
    negs = jnp.pad(neg_row, ((0, 7), (0, 128 - neg_row.shape[1])))

    smem = pltpu.SMEM
    vmem = pl.BlockSpec(memory_space=pltpu.VMEM)
    dma = pltpu.SemaphoreType.DMA
    chunks = 16
    grads, losses = pl.pallas_call(
        functools.partial(kernel, owners, holders, room, chunks, neg_row.shape[1]),
        out_shape=[
            jax.ShapeDtypeStruct((count, tokens, dim), F32),
            jax.ShapeDtypeStruct((count, 128), F32),
        ],
        in_specs=[vmem] * 5 + [pl.BlockSpec(memory_space=pl.ANY)],
        out_specs=[vmem, vmem],
        scratch_shapes=[
            pltpu.VMEM(index.shape, BF16),
            pltpu.VMEM((passages, dim, index.shape[1]), BF16),
            pltpu.VMEM((passages, 128), F32),
            pltpu.VMEM((owners, count, tokens, dim), BF16),
            pltpu.VMEM((count, tokens, dim), BF16),
            pltpu.VMEM((dim, width), BF16),
            pltpu.VMEM((room + 1, tokens, dim), BF16),
            pltpu.VMEM((room + 1, tokens, dim), BF16),
            pltpu.VMEM((room + 8, 128), F32),
            pltpu.VMEM((room + 8, 128), F32),
            pltpu.VMEM((dim, width), F32),
            pltpu.VMEM((8, width), F32),
            pltpu.VMEM((count, tokens, dim), F32),
            pltpu.VMEM((count, tokens, dim), F32),
            pltpu.VMEM((2, count, 128), F32),
            pltpu.VMEM((128, 128), F32),
            pltpu.VMEM((128, 128), F32),
            pltpu.VMEM((count * listed // 128, 128, 128), F32),
            pltpu.VMEM((count * listed // 128, 128, 128), F32),
            pltpu.VMEM((count * listed // 128, 128, 128), F32),
            pltpu.VMEM((owners, 8, 128), I32),
            pltpu.VMEM((owners, 8, 128), F32),
            pltpu.VMEM((owners, 8, 128), I32),
            pltpu.VMEM((owners, 8, 128), F32),
            pltpu.VMEM((holders, 8, 128), I32),
            pltpu.VMEM((owners, count, 2 * tokens, dim), BF16),
            pltpu.VMEM((owners, 2, count, 128), F32),
            pltpu.VMEM((owners, count, 2 * tokens, dim), BF16),
            pltpu.VMEM((owners, 2, count, 128), F32),
            smem((owners, 8, 128), I32),
            smem((owners, 8, 128), F32),
            smem((holders, 8, 128), I32),
            dma((chunks,)),
            *[dma((owners,)) for _ in range(6)],
            *[dma((holders,)) for _ in range(2)],
            *[dma((owners,)) for _ in range(4)],
            dma((3,)),
        ],
        compiler_params=pltpu.CompilerParams(
            collective_id=0, has_side_effects=True, vmem_limit_bytes=60 << 20
        ),
        name="distill",
    )(
        cand_owner.reshape(count, listed), cand_row, negs, teacher,
        queries.reshape(width, dim), index,
    )
    return losses[:, 0], grads


def solution(mesh):
    both = ("corpus", "blk")
    return jax.shard_map(
        step,
        mesh=mesh,
        in_specs=(
            P(both, None, None), P("corpus", None, None), P(both, None, None),
            P(both, None), P(both, None), P(both, None),
        ),
        out_specs=(P(both), P(both, None, None)),
        check_vma=False,
    )
```

time: 217 us -> 181 us (0.83)
  the two profiles are of different devices: /device:TPU:0 before, /device:TPU:14 now
where the time goes in v2:
time: 181 us; the launch traced here: 180 us
  Pallas kernels  175 us (97%)
  local copies, waits for them, and re-layouts  4.25 us (2%)
    pallas_call x1, Pallas kernels, step(): pl.pallas_call(functools.partial(kernel, owners, holders, room, chunks, n...  175 us

profile of v2, /device:TPU:14, one launch (start us, length us, event | category | flops | bytes accessed | tf_op | source)
XLA Modules:
  0.0 180.3 jit_solution(2799725989081140985)
XLA Ops:
  0.6 1.3 pad.4.neg_ref
  1.9 175.4 %distill.1 = (f32[16,32,128]{2,1,0:T(8,128)}, f32[16,128]{1,0:T(8,128)}) custom-call(s32[16,64]{1,0:T(8,128)} %bitcast.3, s32[16,64]{1,0:T(8,128)} %row_ref.1, s32[8,128]{1,0:T(8,128)} %pad.4.neg_ref, f32[16,64]{1,0:T(8,128)} %teacher_ref.1, bf16[512,128]{1,0:T(8,128)(2,1)} %bitcast.2, bf16[512,128,128]{2,1,0:T(8,128)(2,1)} %index_ref.1), custom_call_target="tpu_custom_call" | custom-call | tf_op jit(solution)/shard_map/distill/pallas_call | solution.py:379
  177.3 1.3 slice_reduce_fusion
  178.6 1.7 copy.9

commit v3 on v2

--- a/solution.py
+++ b/solution.py
@@ -106,11 +106,9 @@
     lax.fori_loop(0, owners, one_owner, 0)
 
 
-def negatives(unroll, rows_ref, holders, each, tt_ref, qt_ref, acc_ref, sum_ref):
+def negatives(first_step, last_step, unroll, rows_ref, each, tt_ref, qt_ref, acc_ref, sum_ref):
     width = qt_ref.shape[1]
     lane = lax.broadcasted_iota(I32, (1, width), 1)
-    acc_ref[...] = jnp.zeros_like(acc_ref)
-    sum_ref[...] = jnp.zeros_like(sum_ref)
     steps = each // unroll
 
     def body(b, _):
@@ -134,7 +132,7 @@
         sum_ref[0:1] += jnp.sum(top, axis=0, keepdims=True)
         return 0
 
-    lax.fori_loop(0, holders * steps, body, 0)
+    lax.fori_loop(first_step, last_step, body, 0)
 
 
 def paired_dots(left, right):
@@ -193,7 +191,7 @@
     names_ref, row_ref, neg_ref, teacher_ref, q_ref, index_ref,
     grad_ref, loss_ref,
     w, tt, inv, qall, qcur, qt, pa, pb, p1, p2, acc, nsum, flat_a, flat_s, stats,
-    turned, ends, place, codes, wants, tab_i, tab_f, all_i, all_f, all_n,
+    turned, ends, place, codes, wants, tab_i, tab_f, all_i, all_f, all_n, neg_own,
     back_buf, sum_buf, got, got_sum,
     code_s, mark_s, rows_s,
     load_sem, q_send, q_recv, i_send, i_recv, f_send, f_recv, n_send, n_recv,
@@ -216,8 +214,22 @@
         rows = pl.ds(j * part, part)
         return pltpu.make_async_copy(index_ref.at[rows], w.at[rows], load_sem.at[j])
 
-    def owner(k):
-        return {"corpus": lax.rem(me + k, owners)}
+    side = math.isqrt(owners)
+    own = owners // 2
+
+    def shifted(m, sign):
+        dy = side // 2 + m // side
+        dz = dy + lax.rem(m, side)
+        y = lax.rem(me // side + sign * lax.rem(dy, side) + side, side)
+        z = lax.rem(lax.rem(me, side) + sign * lax.rem(dz, side) + side, side)
+        return y * side + z
+
+    def owner(m):
+        return {"corpus": shifted(m, 1)}
+
+    def peers(act):
+        each(0, own, act)
+        each(own + 1, owners, act)
 
     def holder(k):
         return {"blk": lax.rem(seat + k, holders)}
@@ -232,7 +244,7 @@
         pl.semaphore_signal(barrier, inc=1, device_id=device, device_id_type=MESH)
 
     each(0, chunks, lambda j: loads(j).start())
-    each(1, owners, lambda k: greet(owner(k)))
+    peers(lambda k: greet(owner(k)))
     each(1, holders, lambda k: greet(holder(k)))
 
     wide = q_ref[...].astype(F32)
@@ -241,25 +253,27 @@
     qcur[...] = rounded.reshape(qcur.shape)
     qall[me] = rounded.reshape(qcur.shape)
     qt[...] = jnp.transpose(rounded)
-    all_n[seat] = neg_ref[...]
+    neg_own[...] = jnp.zeros_like(neg_own)
+    neg_own[0:1, 0:sampled] = neg_ref[...]
+    all_n[seat] = neg_own[...]
 
     pl.semaphore_wait(barrier, owners + holders - 2)
 
     def n_copy(k):
-        return remote(neg_ref, all_n.at[seat], n_send, n_recv, k, holder(k))
+        return remote(neg_own, all_n.at[seat], n_send, n_recv, k, holder(k))
 
     def q_copy(k):
         return remote(qcur, qall.at[me], q_send, q_recv, k, owner(k))
 
     def table_copies(k):
-        to = lax.rem(me + k, owners)
+        to = shifted(k, 1)
         return (
             remote(tab_i.at[to], all_i.at[me], i_send, i_recv, k, owner(k)),
             remote(tab_f.at[to], all_f.at[me], f_send, f_recv, k, owner(k)),
         )
 
     each(1, holders, lambda k: n_copy(k).start())
-    each(1, owners, lambda k: q_copy(k).start())
+    peers(lambda k: q_copy(k).start())
 
     teacher = teacher_ref[...]
     log_target = teacher - jnp.log(jnp.sum(jnp.exp(teacher), axis=1, keepdims=True))
@@ -271,7 +285,7 @@
     )
     all_i[me] = tab_i[me]
     all_f[me] = tab_f[me]
-    each(1, owners, lambda k: [copy.start() for copy in table_copies(k)])
+    peers(lambda k: [copy.start() for copy in table_copies(k)])
 
     def prepare(j):
         loads(j).wait()
@@ -279,7 +293,7 @@
 
     each(0, chunks, prepare)
     each(1, holders, lambda k: n_copy(k).wait())
-    each(1, owners, lambda k: [copy.wait() for copy in table_copies(k)])
+    peers(lambda k: [copy.wait() for copy in table_copies(k)])
     moves = [
         pltpu.make_async_copy(all_n, rows_s, smem_sem.at[0]),
         pltpu.make_async_copy(all_i, code_s, smem_sem.at[1]),
@@ -289,8 +303,12 @@
         move.start()
     for move in moves:
         move.wait()
-    negatives(8, rows_s, holders, sampled, tt, qt, acc, nsum)
-    each(1, owners, lambda k: q_copy(k).wait_send())
+    acc[...] = jnp.zeros_like(acc)
+    nsum[...] = jnp.zeros_like(nsum)
+    neg_steps = holders * sampled // 8
+    early = neg_steps // 3
+    negatives(0, early, 8, rows_s, sampled, tt, qt, acc, nsum)
+    peers(lambda k: q_copy(k).wait_send())
 
     pa[room] = jnp.zeros((tokens, 128), BF16)
     pb[room] = jnp.zeros((tokens, 128), BF16)
@@ -298,16 +316,16 @@
     p2[room : room + 8] = jnp.zeros((8, 128), F32)
 
     def back_copies(k):
-        to = {"corpus": lax.rem(me + owners - k, owners)}
+        to = {"corpus": shifted(k, -1)}
         return (
             remote(back_buf.at[k], got.at[k], b_send, b_recv, k, to),
             remote(sum_buf.at[k], got_sum.at[k], s_send, s_recv, k, to),
         )
 
     def source(k):
-        src = lax.rem(me + owners - k, owners)
-
-        @pl.when(k > 0)
+        src = shifted(k, -1)
+
+        @pl.when(k != own)
         def _():
             q_copy(k).wait_recv()
 
@@ -324,43 +342,48 @@
 
         lax.fori_loop(0, count, extract, 0, unroll=4)
 
-        @pl.when(k > 0)
+        @pl.when(k != own)
         def _():
             for copy in back_copies(k):
                 copy.start()
 
     each(0, owners, source)
+    negatives(early, neg_steps, 8, rows_s, sampled, tt, qt, acc, nsum)
 
     turned_a = jnp.transpose(acc[...]) * (1.0 / SCALE)
     turned_s = jnp.transpose(jnp.broadcast_to(nsum[0:1], (128, count * tokens)))
     flat_a[...] = turned_a.reshape(flat_a.shape)
     flat_s[...] = turned_s.reshape(flat_s.shape)
 
-    each(1, owners, lambda k: [copy.wait() for copy in back_copies(k)])
-    sums = sum_buf[0]
-    for k in range(1, owners):
+    peers(lambda k: [copy.wait() for copy in back_copies(k)])
+    sums = sum_buf[own]
+    others = [k for k in range(owners) if k != own]
+    for k in others:
         sums = sums + got_sum[k]
     p1[0:count] = sums[0]
     p2[0:count] = sums[1]
 
     def finish(q, _):
-        part_a = flat_a[q] + back_buf[0, q, 0:tokens].astype(F32)
-        part_b = back_buf[0, q, tokens : 2 * tokens].astype(F32)
-        for k in range(1, owners):
+        part_a = flat_a[q] + back_buf[own, q, 0:tokens].astype(F32)
+        part_b = back_buf[own, q, tokens : 2 * tokens].astype(F32)
+        for k in others:
             part_a = part_a + got[k, q, 0:tokens].astype(F32)
             part_b = part_b + got[k, q, tokens : 2 * tokens].astype(F32)
         whole = flat_s[q] + p1[pl.ds(q, 1)]
         pulled = part_a / whole - part_b
-        own = q_ref[pl.ds(pl.multiple_of(q * tokens, tokens), tokens)].astype(F32)
-        rad = jnp.sqrt(jnp.sum(own * own, axis=-1, keepdims=True) + EPS)
-        unit = own / rad
+        raw = q_ref[pl.ds(pl.multiple_of(q * tokens, tokens), tokens)].astype(F32)
+        rad = jnp.sqrt(jnp.sum(raw * raw, axis=-1, keepdims=True) + EPS)
+        unit = raw / rad
         along = jnp.sum(unit * pulled, axis=-1, keepdims=True)
         grad_ref[q] = (pulled - unit * along) / rad
         one = pl.ds(q, 1)
-        loss_ref[one] = stats[0, one] - LN2 * p2[one] + jnp.log(whole[0:1]) * stats[1, one]
+        stats[2, one] = stats[0, one] - LN2 * p2[one] + jnp.log(whole[0:1]) * stats[1, one]
         return 0
 
     lax.fori_loop(0, count, finish, 0, unroll=2)
+    turned[...] = jnp.zeros_like(turned)
+    turned[0:count] = stats[2]
+    loss_ref[...] = jnp.transpose(turned[...])[0:1, 0:count]
 
 
 def step(queries, index, cand_owner, cand_row, neg_row, teacher):
@@ -370,8 +393,6 @@
     room = 2 * count * listed // owners
     passages = index.shape[0]
     width = count * tokens
-    negs = jnp.pad(neg_row, ((0, 7), (0, 128 - neg_row.shape[1])))
-
     smem = pltpu.SMEM
     vmem = pl.BlockSpec(memory_space=pltpu.VMEM)
     dma = pltpu.SemaphoreType.DMA
@@ -380,7 +401,7 @@
         functools.partial(kernel, owners, holders, room, chunks, neg_row.shape[1]),
         out_shape=[
             jax.ShapeDtypeStruct((count, tokens, dim), F32),
-            jax.ShapeDtypeStruct((count, 128), F32),
+            jax.ShapeDtypeStruct((1, count), F32),
         ],
         in_specs=[vmem] * 5 + [pl.BlockSpec(memory_space=pl.ANY)],
         out_specs=[vmem, vmem],
@@ -399,7 +420,7 @@
             pltpu.VMEM((8, width), F32),
             pltpu.VMEM((count, tokens, dim), F32),
             pltpu.VMEM((count, tokens, dim), F32),
-            pltpu.VMEM((2, count, 128), F32),
+            pltpu.VMEM((3, count, 128), F32),
             pltpu.VMEM((128, 128), F32),
             pltpu.VMEM((128, 128), F32),
             pltpu.VMEM((count * listed // 128, 128, 128), F32),
@@ -410,6 +431,7 @@
             pltpu.VMEM((owners, 8, 128), I32),
             pltpu.VMEM((owners, 8, 128), F32),
             pltpu.VMEM((holders, 8, 128), I32),
+            pltpu.VMEM((8, 128), I32),
             pltpu.VMEM((owners, count, 2 * tokens, dim), BF16),
             pltpu.VMEM((owners, 2, count, 128), F32),
             pltpu.VMEM((owners, count, 2 * tokens, dim), BF16),
@@ -428,10 +450,10 @@
         ),
         name="distill",
     )(
-        cand_owner.reshape(count, listed), cand_row, negs, teacher,
+        cand_owner.reshape(count, listed), cand_row, neg_row, teacher,
         queries.reshape(width, dim), index,
     )
-    return losses[:, 0], grads
+    return losses.reshape(count), grads
 
 
 def solution(mesh):

time: 181 us -> 124 us (0.69)
  the two profiles are of different devices: /device:TPU:14 before, /device:TPU:0 now
where the time goes in v3:
time: 124 us; the launch traced here: 122 us
  Pallas kernels  119 us (96%)
  local copies, waits for them, and re-layouts  2.8 us (2%)
    pallas_call x1, Pallas kernels, step(): pl.pallas_call(functools.partial(kernel, owners, holders, room, chunks, n...  119 us
    unnamed x2, local copies, waits for them, and re-layouts  2.8 us

profile of v3, /device:TPU:0, one launch (start us, length us, event | category | flops | bytes accessed | tf_op | source)
XLA Modules:
  0.0 122.4 jit_solution(14068111996285132088)
XLA Ops:
  0.6 119.0 %distill.1 = (f32[16,32,128]{2,1,0:T(8,128)}, f32[1,16]{1,0:T(1,128)}) custom-call(s32[16,64]{1,0:T(8,128)} %bitcast.4, s32[16,64]{1,0:T(8,128)} %row_ref.1, s32[1,24]{1,0:T(1,128)} %neg_ref.1, f32[16,64]{1,0:T(8,128)} %teacher_ref.1, bf16[512,128]{1,0:T(8,128)(2,1)} %bitcast.3, bf16[512,128,128]{2,1,0:T(8,128)(2,1)} %index_ref.1), custom_call_target="tpu_custom_call" | custom-call | tf_op jit(solution)/shard_map/distill/pallas_call | solution.py:400
  119.6 1.1 copy.10
  120.7 1.7 %copy.11 = f32[16,32,128]{2,1,0:T(8,128)} copy(f32[16,32,128]{2,1,0:T(8,128)} %get-tuple-element.9) | data formatting | bytes 524288

commit v4 on v3

--- a/solution.py
+++ b/solution.py
@@ -153,7 +153,7 @@
     return out
 
 
-def listed_pairs(src, room, unroll, tab_i, tab_f, w_ref, inv_ref, tt_ref, q_ref, pa, pb, p1, p2):
+def listed_pairs(src, room, unroll, group, tab_i, tab_f, w_ref, inv_ref, tt_ref, q_ref, pa, pb, p1, p2):
     zero = jnp.zeros((32, 128), F32)
     one = jnp.zeros((1, 1), F32)
 
@@ -161,26 +161,45 @@
         acc_a, acc_b, acc_1, acc_2 = carry
         ks = [b * unroll + u for u in range(unroll)]
         cs = [tab_i[src, 0, k] for k in ks]
-        sims = paired_dots([q_ref[c & 15] for c in cs], [tt_ref[c >> 4] for c in cs])
-        expo = [jnp.exp2(x) for x in sims]
-        totals = [jnp.sum(x, axis=-1, keepdims=True) for x in expo]
-        weights = [(x * inv_ref[pl.ds(c >> 4, 1)]).astype(BF16) for x, c in zip(expo, cs)]
-        back = paired_dots(weights, [w_ref[c >> 4] for c in cs])
-        logs = [jnp.log2(x) for x in totals]
-        score = [jnp.sum(x, axis=0, keepdims=True) * 0.1 for x in logs]
-        top = [jnp.exp2(x) for x in score]
-        flat = [jnp.exp2(-x) for x in logs]
-        for u, k in enumerate(ks):
-            here = back[u] * flat[u]
-            target, stay = tab_f[src, 0, k], tab_f[src, 1, k]
-            acc_a = acc_a * stay + here * top[u]
-            acc_b = acc_b * stay + here * target
-            acc_1 = acc_1 * stay + top[u]
-            acc_2 = acc_2 * stay + score[u] * target
-            pa[k] = acc_a.astype(BF16)
-            pb[k] = acc_b.astype(BF16)
-            p1[pl.ds(k, 1)] = jnp.broadcast_to(acc_1, (1, 128))
-            p2[pl.ds(k, 1)] = jnp.broadcast_to(acc_2, (1, 128))
+        sims, expo, totals, weights, back, score, top, flat = [{} for _ in range(8)]
+        steps = unroll // group
+        for t in range(steps + 3):
+            us = range(t * group, (t + 1) * group)
+            if t < steps:
+                dots = paired_dots([q_ref[cs[u] & 15] for u in us], [tt_ref[cs[u] >> 4] for u in us])
+                sims.update(zip(us, dots))
+            us = range((t - 1) * group, t * group)
+            if 0 <= t - 1 < steps:
+                for u in us:
+                    expo[u] = jnp.exp2(sims.pop(u))
+                    totals[u] = jnp.sum(expo[u], axis=-1, keepdims=True)
+                for u in us:
+                    weights[u] = (expo.pop(u) * inv_ref[pl.ds(cs[u] >> 4, 1)]).astype(BF16)
+            us = range((t - 2) * group, (t - 1) * group)
+            if 0 <= t - 2 < steps:
+                dots = paired_dots([weights.pop(u) for u in us], [w_ref[cs[u] >> 4] for u in us])
+                back.update(zip(us, dots))
+                logs = {u: jnp.log2(totals.pop(u)) for u in us}
+                for u in us:
+                    flat[u] = jnp.exp2(-logs[u])
+                for u in us:
+                    score[u] = jnp.sum(logs[u], axis=0, keepdims=True) * 0.1
+                for u in us:
+                    top[u] = jnp.exp2(score[u])
+            us = range((t - 3) * group, (t - 2) * group)
+            if 0 <= t - 3 < steps:
+                for u in us:
+                    k = ks[u]
+                    here = back.pop(u) * flat.pop(u)
+                    target, stay = tab_f[src, 0, k], tab_f[src, 1, k]
+                    acc_a = acc_a * stay + here * top[u]
+                    acc_b = acc_b * stay + here * target
+                    acc_1 = acc_1 * stay + top[u]
+                    acc_2 = acc_2 * stay + score[u] * target
+                    pa[k] = acc_a.astype(BF16)
+                    pb[k] = acc_b.astype(BF16)
+                    p1[pl.ds(k, 1)] = jnp.broadcast_to(acc_1, (1, 128))
+                    p2[pl.ds(k, 1)] = jnp.broadcast_to(acc_2, (1, 128))
         return acc_a, acc_b, acc_1, acc_2
 
     lax.fori_loop(0, room // unroll, body, (zero, zero, one, one))
@@ -250,7 +269,6 @@
     wide = q_ref[...].astype(F32)
     radius = jnp.sqrt(jnp.sum(wide * wide, axis=-1, keepdims=True) + EPS)
     rounded = (wide / radius).astype(BF16)
-    qcur[...] = rounded.reshape(qcur.shape)
     qall[me] = rounded.reshape(qcur.shape)
     qt[...] = jnp.transpose(rounded)
     neg_own[...] = jnp.zeros_like(neg_own)
@@ -263,7 +281,7 @@
         return remote(neg_own, all_n.at[seat], n_send, n_recv, k, holder(k))
 
     def q_copy(k):
-        return remote(qcur, qall.at[me], q_send, q_recv, k, owner(k))
+        return remote(qall.at[me], qall.at[me], q_send, q_recv, k, owner(k))
 
     def table_copies(k):
         to = shifted(k, 1)
@@ -306,9 +324,8 @@
     acc[...] = jnp.zeros_like(acc)
     nsum[...] = jnp.zeros_like(nsum)
     neg_steps = holders * sampled // 8
-    early = neg_steps // 3
+    early = 0
     negatives(0, early, 8, rows_s, sampled, tt, qt, acc, nsum)
-    peers(lambda k: q_copy(k).wait_send())
 
     pa[room] = jnp.zeros((tokens, 128), BF16)
     pb[room] = jnp.zeros((tokens, 128), BF16)
@@ -330,7 +347,7 @@
             q_copy(k).wait_recv()
 
         qcur[...] = qall[src]
-        listed_pairs(src, room, 32, code_s, mark_s, w, inv, tt, qcur, pa, pb, p1, p2)
+        listed_pairs(src, room, 64, 8, code_s, mark_s, w, inv, tt, qcur, pa, pb, p1, p2)
 
         def extract(q, _):
             at = code_s[src, 1, q]
@@ -356,6 +373,7 @@
     flat_s[...] = turned_s.reshape(flat_s.shape)
 
     peers(lambda k: [copy.wait() for copy in back_copies(k)])
+    peers(lambda k: q_copy(k).wait_send())
     sums = sum_buf[own]
     others = [k for k in range(owners) if k != own]
     for k in others:

time: 124 us -> 115 us (0.927)
  Pallas kernels: 119 us -> 111 us
    pallas_call x1, Pallas kernels: 119 us -> 111 us  [step(): pl.pallas_call(functools.partial(kernel, owners, holders, room, chunks, n...]
where the time goes in v4:
time: 115 us; the launch traced here: 114 us
  Pallas kernels  111 us (97%)
  local copies, waits for them, and re-layouts  2.8 us (2%)
    pallas_call x1, Pallas kernels, step(): pl.pallas_call(functools.partial(kernel, owners, holders, room, chunks, n...  111 us
    unnamed x2, local copies, waits for them, and re-layouts  2.8 us

profile of v4, /device:TPU:0, one launch (start us, length us, event | category | flops | bytes accessed | tf_op | source)
XLA Modules:
  0.0 114.4 jit_solution(14985623279212436476)
XLA Ops:
  0.6 110.9 %distill.1 = (f32[16,32,128]{2,1,0:T(8,128)}, f32[1,16]{1,0:T(1,128)}) custom-call(s32[16,64]{1,0:T(8,128)} %bitcast.4, s32[16,64]{1,0:T(8,128)} %row_ref.1, s32[1,24]{1,0:T(1,128)} %neg_ref.1, f32[16,64]{1,0:T(8,128)} %teacher_ref.1, bf16[512,128]{1,0:T(8,128)(2,1)} %bitcast.3, bf16[512,128,128]{2,1,0:T(8,128)(2,1)} %index_ref.1), custom_call_target="tpu_custom_call" | custom-call | tf_op jit(solution)/shard_map/distill/pallas_call | solution.py:418
  111.5 1.1 copy.10
  112.7 1.7 %copy.11 = f32[16,32,128]{2,1,0:T(8,128)} copy(f32[16,32,128]{2,1,0:T(8,128)} %get-tuple-element.9) | data formatting | bytes 524288

commit v5 on v4

--- a/solution.py
+++ b/solution.py
@@ -234,11 +234,11 @@
         return pltpu.make_async_copy(index_ref.at[rows], w.at[rows], load_sem.at[j])
 
     side = math.isqrt(owners)
-    own = owners // 2
+    own = side // 2
 
     def shifted(m, sign):
-        dy = side // 2 + m // side
-        dz = dy + lax.rem(m, side)
+        dy = side // 2 + lax.rem(m, side)
+        dz = dy + m // side
         y = lax.rem(me // side + sign * lax.rem(dy, side) + side, side)
         z = lax.rem(lax.rem(me, side) + sign * lax.rem(dz, side) + side, side)
         return y * side + z
@@ -291,7 +291,9 @@
         )
 
     each(1, holders, lambda k: n_copy(k).start())
-    peers(lambda k: q_copy(k).start())
+    at_once = 4
+    each(0, own, lambda k: q_copy(k).start())
+    each(own + 1, at_once, lambda k: q_copy(k).start())
 
     teacher = teacher_ref[...]
     log_target = teacher - jnp.log(jnp.sum(jnp.exp(teacher), axis=1, keepdims=True))
@@ -306,6 +308,10 @@
     peers(lambda k: [copy.start() for copy in table_copies(k)])
 
     def prepare(j):
+        @pl.when(j < owners - at_once)
+        def _():
+            q_copy(at_once + j).start()
+
         loads(j).wait()
         transpose_pass(j * part, part, 8, w, inv, tt)
 

time: 115 us -> 102 us (0.89)
  Pallas kernels: 111 us -> 98.4 us
    pallas_call x1, Pallas kernels: 111 us -> 98.4 us  [step(): pl.pallas_call(functools.partial(kernel, owners, holders, room, chunks, n...]
where the time goes in v5:
time: 102 us
  Pallas kernels  98.4 us (96%)
  local copies, waits for them, and re-layouts  2.8 us (3%)
    pallas_call x1, Pallas kernels, step(): pl.pallas_call(functools.partial(kernel, owners, holders, room, chunks, n...  98.4 us
    unnamed x2, local copies, waits for them, and re-layouts  2.8 us

profile of v5, /device:TPU:0, one launch (start us, length us, event | category | flops | bytes accessed | tf_op | source)
XLA Modules:
  0.0 101.9 jit_solution(3656976516350842667)
XLA Ops:
  0.6 98.4 %distill.1 = (f32[16,32,128]{2,1,0:T(8,128)}, f32[1,16]{1,0:T(1,128)}) custom-call(s32[16,64]{1,0:T(8,128)} %bitcast.4, s32[16,64]{1,0:T(8,128)} %row_ref.1, s32[1,24]{1,0:T(1,128)} %neg_ref.1, f32[16,64]{1,0:T(8,128)} %teacher_ref.1, bf16[512,128]{1,0:T(8,128)(2,1)} %bitcast.3, bf16[512,128,128]{2,1,0:T(8,128)(2,1)} %index_ref.1), custom_call_target="tpu_custom_call" | custom-call | tf_op jit(solution)/shard_map/distill/pallas_call | solution.py:424
  99.1 1.1 %copy.10 = f32[16]{0:T(128)} copy(f32[16]{0:T(128)} %bitcast.5) | data formatting | bytes 128
  100.2 1.7 %copy.11 = f32[16,32,128]{2,1,0:T(8,128)} copy(f32[16,32,128]{2,1,0:T(8,128)} %get-tuple-element.9) | data formatting | bytes 524288

commit v6 on v5

--- a/solution.py
+++ b/solution.py
@@ -329,9 +329,9 @@
         move.wait()
     acc[...] = jnp.zeros_like(acc)
     nsum[...] = jnp.zeros_like(nsum)
-    neg_steps = holders * sampled // 8
+    neg_steps = holders * sampled // 12
     early = 0
-    negatives(0, early, 8, rows_s, sampled, tt, qt, acc, nsum)
+    negatives(0, early, 12, rows_s, sampled, tt, qt, acc, nsum)
 
     pa[room] = jnp.zeros((tokens, 128), BF16)
     pb[room] = jnp.zeros((tokens, 128), BF16)
@@ -371,7 +371,7 @@
                 copy.start()
 
     each(0, owners, source)
-    negatives(early, neg_steps, 8, rows_s, sampled, tt, qt, acc, nsum)
+    negatives(early, neg_steps, 12, rows_s, sampled, tt, qt, acc, nsum)
 
     turned_a = jnp.transpose(acc[...]) * (1.0 / SCALE)
     turned_s = jnp.transpose(jnp.broadcast_to(nsum[0:1], (128, count * tokens)))

time: 102 us -> 96.8 us (0.949); the launches traced: 102 us -> 95.6 us
  Pallas kernels: 98.4 us -> 92.2 us
    pallas_call x1, Pallas kernels: 98.4 us -> 92.2 us  [step(): pl.pallas_call(functools.partial(kernel, owners, holders, room, chunks, n...]
where the time goes in v6:
time: 96.8 us; the launch traced here: 95.6 us
  Pallas kernels  92.2 us (95%)
  local copies, waits for them, and re-layouts  2.8 us (3%)
    pallas_call x1, Pallas kernels, step(): pl.pallas_call(functools.partial(kernel, owners, holders, room, chunks, n...  92.2 us
    unnamed x2, local copies, waits for them, and re-layouts  2.8 us

profile of v6, /device:TPU:0, one launch (start us, length us, event | category | flops | bytes accessed | tf_op | source)
XLA Modules:
  0.0 95.6 jit_solution(6331540872375665890)
XLA Ops:
  0.6 92.2 %distill.1 = (f32[16,32,128]{2,1,0:T(8,128)}, f32[1,16]{1,0:T(1,128)}) custom-call(s32[16,64]{1,0:T(8,128)} %bitcast.4, s32[16,64]{1,0:T(8,128)} %row_ref.1, s32[1,24]{1,0:T(1,128)} %neg_ref.1, f32[16,64]{1,0:T(8,128)} %teacher_ref.1, bf16[512,128]{1,0:T(8,128)(2,1)} %bitcast.3, bf16[512,128,128]{2,1,0:T(8,128)(2,1)} %index_ref.1), custom_call_target="tpu_custom_call" | custom-call | tf_op jit(solution)/shard_map/distill/pallas_call | solution.py:424
  92.8 1.1 %copy.10 = f32[16]{0:T(128)} copy(f32[16]{0:T(128)} %bitcast.5) | data formatting | bytes 128
  93.9 1.7 %copy.11 = f32[16,32,128]{2,1,0:T(8,128)} copy(f32[16,32,128]{2,1,0:T(8,128)} %get-tuple-element.9) | data formatting | bytes 524288
